TPU v7x, 256 devices: a whole 4x4x8 slice. The times are simulated.
256 devices in a mesh: row: 16 (over x_lo, z), col: 16 (over x_hi, y, core).
Axes of the slice: x: 4 (x_hi: 2, x_lo: 2; x = x_hi * 2 + x_lo), y: 4, z: 8, core: 2. Of those that a mesh axis runs over, the one named last changes fastest.
Arguments:
- hidden_in: bfloat16 [12288, 5120], P('row', 'col'), may hold values from -6 to 6
- modulation: bfloat16 [48, 3, 5120], P(None, None, 'col'), may hold values from -3 to 3
- w_qkv: bfloat16 [5120, 12288], P('row', 'col'), may hold values from -0.078125 to 0.078125
- w_out: bfloat16 [4096, 5120], P('row', 'col'), may hold values from -0.09375 to 0.09375
- prefix_cache: bfloat16 [16, 256, 8192], P('row', None, 'col'), may hold values from -48 to 48
- req_group: int32 [48], replicated, may hold values from 0 to 3
- req_len: int32 [48], replicated, may hold values from 1 to 672, 12288 in all
- owner: int32 [4], replicated, may hold values from 0 to 15, as said below
Outputs:
- hidden_out: bfloat16 [12288, 5120], P('row', 'col')
- suffix_keys: bfloat16 [12288, 4096], P('row', 'col')
- suffix_values: bfloat16 [12288, 4096], P('row', 'col')
Inputs may be any that keep to these rules, and one draw needn't show every extreme that they name: `owner`: the 4 slots are distinct; slot 0 and slot 16 - 1 always hold a group.
All inputs are finite; a program needn't handle non-finite values.
Results may differ from a plain program's by a relative error of at most 0.006.
Values may be sent and summed in bfloat16 or wider, within the bound.
A program may use at most 192 MiB of HBM per device.

v0:
```python
import math

import jax
import jax.numpy as jnp
from jax import lax
from jax.sharding import PartitionSpec as P

HD = 128


neg_fill = -1e30


def with_halo(block, sides, width):
    for axis, dim in sides:
        count = lax.axis_size(axis)
        forward = [(i, i + 1) for i in range(count - 1)]
        backward = [(target, source) for source, target in forward]
        low = lax.ppermute(
            lax.slice_in_dim(block, block.shape[dim] - width, None, axis=dim), axis, forward
        )
        high = lax.ppermute(lax.slice_in_dim(block, 0, width, axis=dim), axis, backward)
        block = jnp.concatenate([low, block, high], axis=dim)
    return block


def request_of(positions, req_len):
    starts = jnp.cumsum(req_len) - req_len
    inside = (starts[None, :] <= positions[:, None]).astype(jnp.int32)
    return jnp.sum(inside, axis=1) - 1


def attend(running, queries, key_block, value_block, allowed):
    largest, denominator, summed = running
    scores = jnp.einsum("thd,khd->thk", queries, key_block, preferred_element_type=jnp.float32)
    scores = scores * (1.0 / math.sqrt(queries.shape[-1]))
    widened = allowed[:, None, :]
    scores = jnp.where(widened, scores, neg_fill)
    new_largest = jnp.maximum(largest, jnp.max(scores, axis=2))
    weights = jnp.where(widened, jnp.exp(scores - new_largest[:, :, None]), 0.0)
    rescale = jnp.exp(largest - new_largest)
    denominator = denominator * rescale + jnp.sum(weights, axis=2)
    summed = summed * rescale[:, :, None] + jnp.einsum(
        "thk,khd->thd",
        weights.astype(jnp.bfloat16),
        value_block,
        preferred_element_type=jnp.float32,
    )
    return (new_largest, denominator, summed)


def shards(hidden_in, modulation, w_qkv, w_out, prefix_cache, req_group, req_len, owner):
    token_rows = hidden_in.shape[0]
    full_hidden, full_modulation = (
        lax.all_gather(hidden_in, "col", axis=1, tiled=True),
        lax.all_gather(modulation, "col", axis=2, tiled=True),
    )
    full_width = full_hidden.shape[1]
    requests = req_len.shape[0]
    row_index = lax.axis_index("row")
    positions = row_index * token_rows + jnp.arange(token_rows, dtype=jnp.int32)
    request_id = request_of(positions, req_len)
    matches = request_id[:, None] == jnp.arange(requests, dtype=jnp.int32)[None, :]
    onehot = matches.astype(jnp.bfloat16)
    per_token = jnp.dot(
        onehot,
        full_modulation.reshape(requests, 3 * full_width),
        preferred_element_type=jnp.float32,
    )
    shift_rows = per_token[:, :full_width]
    scale_rows = per_token[:, full_width : 2 * full_width]
    gate_rows = jnp.dot(onehot, modulation[:, 2, :], preferred_element_type=jnp.float32)
    token_group = jnp.sum(jnp.where(matches, req_group[None, :], 0), axis=1)
    hidden_f = full_hidden.astype(jnp.float32)
    average = jnp.mean(hidden_f, axis=1, keepdims=True)
    centred = hidden_f - average
    variance = jnp.mean(centred * centred, axis=1, keepdims=True)
    modulated = (centred * lax.rsqrt(variance + 1e-06) * (1.0 + scale_rows) + shift_rows).astype(
        jnp.bfloat16
    )
    projected_qkv = jnp.dot(
        modulated,
        lax.all_gather(w_qkv, "row", axis=0, tiled=True),
        preferred_element_type=jnp.float32,
    )
    local_heads = w_qkv.shape[1] // (3 * HD)
    projected_qkv = projected_qkv.astype(jnp.bfloat16).reshape(token_rows, local_heads, 3, HD)
    queries = projected_qkv[:, :, 0]
    new_keys = projected_qkv[:, :, 1]
    new_values = projected_qkv[:, :, 2]
    key_value = projected_qkv[:, :, 1:].reshape(token_rows, local_heads * 2 * HD)
    surrounded = with_halo(key_value, (("row", 0),), token_rows)
    running = (
        jnp.full((token_rows, local_heads), neg_fill, jnp.float32),
        jnp.zeros((token_rows, local_heads), jnp.float32),
        jnp.zeros((token_rows, local_heads, HD), jnp.float32),
    )

    def slot_attend(carried, slot_data, group_number):
        present = token_group == group_number
        arranged = slot_data.reshape(slot_data.shape[0], local_heads, 2, HD)
        allowed = jnp.broadcast_to(present[:, None], (token_rows, slot_data.shape[0]))
        return attend(carried, queries, arranged[:, :, 0], arranged[:, :, 1], allowed)

    group_numbers = jnp.arange(owner.shape[0], dtype=jnp.int32)
    slot_block = lax.all_gather(prefix_cache, "row", axis=0, tiled=True)

    def one_slot(offset, current):
        group_number = jnp.sum(jnp.where(owner == offset, group_numbers + 1, 0)) - 1
        slot_data = lax.dynamic_index_in_dim(slot_block, offset, 0, keepdims=False)
        return slot_attend(current, slot_data, group_number)

    running = lax.fori_loop(0, slot_block.shape[0], one_slot, running)
    near_pairs = surrounded.reshape(3 * token_rows, local_heads, 2, HD)
    key_pos = (row_index - 1) * token_rows + jnp.arange(3 * token_rows, dtype=jnp.int32)
    key_req = request_of(key_pos, req_len)
    inside_range = key_pos < jnp.sum(req_len)
    near_mask = (key_req[None, :] == request_id[:, None]) & inside_range[None, :]
    running = attend(running, queries, near_pairs[:, :, 0], near_pairs[:, :, 1], near_mask)
    largest, denominator, summed = running
    attended = (
        (summed / denominator[:, :, None])
        .astype(jnp.bfloat16)
        .reshape(token_rows, local_heads * HD)
    )
    out_weight = lax.all_gather(w_out, "row", axis=0, tiled=True)
    projected = jnp.dot(
        lax.all_gather(attended, "col", axis=1, tiled=True),
        out_weight,
        preferred_element_type=jnp.float32,
    )
    hidden_out = (hidden_in.astype(jnp.float32) + gate_rows * projected).astype(jnp.bfloat16)
    return (
        hidden_out,
        new_keys.reshape(token_rows, local_heads * HD),
        new_values.reshape(token_rows, local_heads * HD),
    )


def solution(mesh):
    return jax.shard_map(
        shards,
        mesh=mesh,
        in_specs=(
            P("row", "col"),
            P(None, None, "col"),
            P("row", "col"),
            P("row", "col"),
            P("row", None, "col"),
            P(),
            P(),
            P(),
        ),
        out_specs=(P("row", "col"), P("row", "col"), P("row", "col")),
        check_vma=False,
    )
```

profile of v0, /device:TPU:1, one launch (start us, length us, event | category | flops | bytes accessed | tf_op | source)
XLA Modules:
  0.0 497.8 jit_solution(4544151833377507003)
XLA Ops:
  7.2 1.8 copy.59
  15.7 2.9 compare_and_fusion
  18.6 61.9 %all-gather.11.cloned.1.call-done = bf16[48,3,5120]{0,1,2:T(4,128)(2,1)} async-done(((bf16[48,3,320]{0,1,2:T(4,128)(2,1)}), bf16[48,3,5120]{0,1,2:T(4,128)(2,1)}) %all-gather.11.cloned.1.call-update) | async-done | bytes 1474576 | tf_op jit(solution)/shard_map/all_gather | solution.py:56
  80.4 7.7 %copy.60 = bf16[48,3,5120]{2,1,0:T(4,128)(2,1)S(1)} copy(bf16[48,3,5120]{0,1,2:T(4,128)(2,1)} %all-gather.11.cloned.1.call-done) | data formatting | bytes 2949120 | tf_op jit(solution)/shard_map/all_gather | solution.py:56
  88.8 18.8 %fusion.48 = f32[768,15360]{1,0:T(8,128)} fusion(bf16[48,15360]{1,0:T(8,128)(2,1)S(1)} %bitcast.111, s32[768]{0:T(1024)S(1)} %broadcast_add_fusion.1), kind=kOutput, calls=%fused_computation.61 | convolution fusion | flops 1132498944 | bytes 48663552 | tf_op jit(solution)/shard_map/dot_general | solution.py:65
  107.5 49.4 %all-gather.9.cloned.1.call-done = bf16[768,5120]{0,1:T(8,128)(2,1)} async-done(((bf16[768,320]{0,1:T(8,128)(2,1)}), bf16[768,5120]{0,1:T(8,128)(2,1)}) %all-gather.9.cloned.1.call-update) | async-done | bytes 7864336 | tf_op jit(solution)/shard_map/all_gather | solution.py:55
  156.9 10.7 %copy.58 = bf16[768,5120]{1,0:T(8,128)(2,1)} copy(bf16[768,5120]{0,1:T(8,128)(2,1)} %all-gather.9.cloned.1.call-done) | data formatting | bytes 15728640 | tf_op jit(solution)/shard_map/all_gather | solution.py:55
  167.6 4.5 convert_reduce_fusion
  173.1 2.2 fusion.17
  175.3 76.6 %all-gather.13.cloned.1.call-done = bf16[5120,768]{1,0:T(8,128)(2,1)} async-done(((bf16[320,768]{1,0:T(8,128)(2,1)}), bf16[5120,768]{1,0:T(8,128)(2,1)}) %all-gather.13.cloned.1.call-update) | async-done | bytes 7864336 | tf_op jit(solution)/shard_map/all_gather | solution.py:83
  251.9 21.3 %fusion.29 = bf16[768,768]{0,1:T(8,128)(2,1)S(1)} fusion(bf16[5120,768]{1,0:T(8,128)(2,1)} %all-gather.13.cloned.1.call-done, bf16[768,5120]{1,0:T(8,128)(2,1)} %copy.58, f32[768,15360]{1,0:T(8,128)} %fusion.48, f32[768]{0:T(1024)S(1)} %add_rsqrt_fusion, f32[768]{0:T(1024)S(1)} %broadcast_multiply_fusion), kind=kOutput, calls=%fused_computation.46 | convolution fusion | flops 6067912704 | bytes 48371712 | tf_op jit(solution)/shard_map/dot_general | solution.py:81
  274.3 2.2 collective-permute-start
  276.4 1.5 collective-permute-start.1
  279.1 51.5 %all-gather.7.cloned.1.call-done = bf16[16,256,512]{2,1,0:T(8,128)(2,1)} async-done(((bf16[1,256,512]{2,1,0:T(8,128)(2,1)}), bf16[16,256,512]{2,1,0:T(8,128)(2,1)}) %all-gather.7.cloned.1.call-update) | async-done | bytes 4194320 | tf_op jit(solution)/shard_map/all_gather | solution.py:106
  330.6 58.0 %while.20 = (s32[]{:T(128)}, f32[768,2]{0,1:T(2,128)S(1)}, f32[768,2]{0,1:T(2,128)S(1)}, f32[768,2,128]{0,2,1:T(8,128)S(1)}, s32[4]{0:T(128)S(1)}, /*index=5*/s3...) while((s32[]{:T(128)}, f32[768,2]{0,1:T(2,128)S(1)}, ...), condition=%wide.region_9.10_spmd.clone, body=%wide.region_5.9_spmd.clone.sunk | while | flops 205463824 | bytes 8100517 | solution.py:113
  388.6 1.6 copy.80
  390.3 2.3 copy.65
  392.6 2.3 copy.66
  394.9 1.5 pad_maximum_fusion
  396.4 4.2 fusion.21
  400.7 4.0 fusion.22
  404.7 5.7 %fusion.44 = bf16[768,2,128]{0,2,1:T(8,128)(2,1)} fusion(f32[2,2304,768]{2,1,0:T(8,128)S(1)} %get-tuple-element.301, f32[768,2]{0,1:T(2,128)S(1)} %max.13, pred[768,2304]{0,1:T(8,128)(4,1)S(1)} %copy-done.1, bf16[2304,2,2,128]{3,0,1,2:T(8,128)(2,1)} %copy-done.3, f32[768,2,128]{0,2,1:T(8,128)S(1)} %get-tuple-element.225, ...), kind=kOutput, calls=%fused_computation.56 | convolution fusion | flops 924450816 | bytes 18302976 | tf_op jit(solution)/shard_map/thk,khd->thd/dot_general | solution.py:43
  413.4 71.0 %all-gather.15.cloned.1.call-done = bf16[768,4096]{0,1:T(8,128)(2,1)} async-done(((bf16[768,256]{0,1:T(8,128)(2,1)}), bf16[768,4096]{0,1:T(8,128)(2,1)}) %all-gather.15.cloned.1.call-update) | async-done | bytes 6291472 | tf_op jit(solution)/shard_map/all_gather | solution.py:128
  484.4 6.6 %fusion.36 = bf16[768,320]{0,1:T(8,128)(2,1)} fusion(f32[768,320]{0,1:T(8,128)S(1)} %fusion.49, bf16[4096,320]{0,1:T(8,128)(2,1)} %all-gather.17.cloned.1.call-done, bf16[768,4096]{0,1:T(8,128)(2,1)} %all-gather.15.cloned.1.call-done, bf16[768,320]{0,1:T(8,128)(2,1)} %param.10), kind=kOutput, calls=%fused_computation.50 | convolution fusion | flops 2014248960 | bytes 10878976 | tf_op jit(solution)/shard_map/dot_general | solution.py:127
  (215 shorter events, 61.0 us)
Async XLA Ops:
  7.2 73.3 %all-gather.11.cloned.1.call-start = ((), (), s32[]{:S(2)}) async-start(), calls=%async_computation.2 | async-start | bytes 5570560 | tf_op jit(solution)/shard_map/all_gather | solution.py:56
  9.1 147.9 %all-gather.9.cloned.1.call-start = ((), (), s32[]{:S(2)}) async-start(), calls=%async_computation.1 | async-start | bytes 8355840 | tf_op jit(solution)/shard_map/all_gather | solution.py:55
  9.8 242.1 %all-gather.13.cloned.1.call-start = ((), (), s32[]{:S(2)}) async-start(), calls=%async_computation.3 | async-start | bytes 8355840 | tf_op jit(solution)/shard_map/all_gather | solution.py:83
  10.5 320.1 %all-gather.7.cloned.1.call-start = ((), (), s32[]{:S(2)}) async-start(), calls=%async_computation | async-start | bytes 4456448 | tf_op jit(solution)/shard_map/all_gather | solution.py:106
  11.1 402.3 %all-gather.17.cloned.1.call-start = ((), (), s32[]{:S(2)}) async-start(), calls=%async_computation.5 | async-start | bytes 2785280 | tf_op jit(solution)/shard_map/all_gather | solution.py:126
  11.7 472.7 %all-gather.15.cloned.1.call-start = ((), (), s32[]{:S(2)}) async-start(), calls=%async_computation.4 | async-start | bytes 6684672 | tf_op jit(solution)/shard_map/all_gather | solution.py:128
  167.6 5.5 %copy-start = (bf16[768,5120]{1,0:T(8,128)(2,1)S(1)}, bf16[768,5120]{1,0:T(8,128)(2,1)}, u32[]{:S(2)}) copy-start(bf16[768,5120]{1,0:T(8,128)(2,1)} %copy.58) | copy-start | bytes 23592964
  175.3 155.3 %copy-start.6 = (s32[4]{0:T(128)S(1)}, s32[4]{0:T(128)}, u32[]{:S(2)}) copy-start(s32[4]{0:T(128)} %param.17) | copy-start | bytes 52
  273.2 5.6 %copy-start.2 = (bf16[768,768]{0,1:T(8,128)(2,1)}, bf16[768,768]{0,1:T(8,128)(2,1)S(1)}, u32[]{:S(2)}) copy-start(bf16[768,768]{0,1:T(8,128)(2,1)S(1)} %fusion.29) | copy-start | bytes 3538948
  274.3 116.0 %collective-permute-start = (bf16[768,512]{0,1:T(8,128)(2,1)}, bf16[768,512]{0,1:T(8,128)(2,1)}, u32[]{:S(2)}, u32[]{:S(2)}) collective-permute-start(bf16[768,512]{0,1:T(8,128)(2,1)} %bitcast.4), channel_id=1, source_target_pairs={{0,16},{16,32},{32,48},{48,64},{64,80},{80,96},{96,112},{112,128},... | collective-permute-start | bytes 2359304 | tf_op jit(solution)/shard_map/ppermute | solution.py:19
  276.4 116.2 %collective-permute-start.1 = (bf16[768,512]{0,1:T(8,128)(2,1)}, bf16[768,512]{0,1:T(8,128)(2,1)}, u32[]{:S(2)}, u32[]{:S(2)}) collective-permute-start(bf16[768,512]{0,1:T(8,128)(2,1)} %bitcast.4), channel_id=1, source_target_pairs={{16,0},{32,16},{48,32},{64,48},{80,64},{96,80},{112,96},{128,112},... | collective-permute-start | bytes 2359304 | tf_op jit(solution)/shard_map/ppermute | solution.py:22
  388.6 7.8 %copy-start.1 = (pred[768,2304]{0,1:T(8,128)(4,1)S(1)}, pred[768,2304]{0,1:T(8,128)(4,1)}, u32[]{:S(2)}) copy-start(pred[768,2304]{0,1:T(8,128)(4,1)} %compare_and_fusion) | copy-start | bytes 5308420
  396.4 4.2 copy-start.3
  404.7 6.9 %copy-start.5 = (bf16[768,2,1,128]{0,3,2,1:T(8,128)(2,1)S(1)}, bf16[768,2,1,128]{0,3,2,1:T(8,128)(2,1)}, u32[]{:S(2)}) copy-start(bf16[768,2,1,128]{0,3,2,1:T(8,128)(2,1)} %get-tuple-element.297) | copy-start | bytes 1179652
  404.7 7.8 %copy-start.4 = (bf16[768,2,1,128]{0,3,2,1:T(8,128)(2,1)S(1)}, bf16[768,2,1,128]{0,3,2,1:T(8,128)(2,1)}, u32[]{:S(2)}) copy-start(bf16[768,2,1,128]{0,3,2,1:T(8,128)(2,1)} %get-tuple-element.295) | copy-start | bytes 1179652
Sparse Core Ops, SparseCore 0:
  11.3 69.0 all-gather.10
  83.2 73.6 all-gather.8
  158.7 93.1 all-gather.12
  253.6 77.0 all-gather.6
  332.2 69.7 all-gather.16
  410.6 73.7 all-gather.14
where the time goes:
time: 499 us; the launch traced here: 498 us
  waiting for transfers between devices  313 us (63%)
  matrix products  72.6 us (15%)
  local copies, waits for them, and re-layouts  50.6 us (10%)
  other arithmetic  33.2 us (7%)
  between operations  14.4 us (3%)
  loops' own time  10.3 us (2%)
    all_gather x1, waiting for transfers between devices, shards(): lax.all_gather(w_qkv, 'row', axis=0, tiled=True)  76.6 us
    all_gather x1, waiting for transfers between devices, shards(): lax.all_gather(attended, 'col', axis=1, tiled=True)  71 us
    all_gather x1, waiting for transfers between devices, shards(): lax.all_gather(modulation, 'col', axis=2, tiled=True)  61.9 us
    all_gather x1, waiting for transfers between devices, shards(): slot_block = lax.all_gather(prefix_cache, 'row', axis=0, tiled=True)  51.5 us
    all_gather x1, waiting for transfers between devices, shards(): lax.all_gather(hidden_in, 'col', axis=1, tiled=True)  49.4 us
    dot_general x1, matrix products, shards(): jnp.dot(modulated, lax.all_gather(w_qkv, 'row', axis=0, tiled=True), pref...  21.3 us
    dot_general x1, matrix products, shards(): jnp.dot(onehot, full_modulation.reshape(requests, 3 * full_width), prefer...  18.8 us
    dynamic_slice x32, local copies, waits for them, and re-layouts, one_slot(): slot_data = lax.dynamic_index_in_dim(slot_block, offset, 0, keepdims=False)  17.7 us
  transfers between devices with their start and end apart: 8, of which 5 were waited for; matrix products, arithmetic and copies ran while one was open for 30% of the time, Pallas kernels for 0%

commit v1 on v0

v1 whole, which is shorter than its diff:
```python
import functools
import math

import jax
import jax.numpy as jnp
from jax import lax
from jax.experimental import pallas as pl
from jax.experimental.pallas import tpu as pltpu
from jax.sharding import PartitionSpec as P

HD = 128
N_Z = 8
N_Y = 4
MESH = pl.DeviceIdType.MESH
BIG = 1e30
VMEM_LIMIT = 56 << 20


def contract_first(a, b):
    return lax.dot_general(a, b, (((0,), (0,)), ((), ())), preferred_element_type=jnp.float32)


class Place:
    def __init__(self):
        self.row, self.col = lax.axis_index("row"), lax.axis_index("col")
        self.l, self.z = self.row // N_Z, self.row % N_Z
        self.h, self.y, self.k = self.col // (2 * N_Y), (self.col // 2) % N_Y, self.col % 2

    def row_at(self, plane, dz):
        l = 1 - self.l if plane else self.l
        return l * N_Z + (self.z + dz + N_Z) % N_Z

    def col_at(self, half, dy, core):
        h = 1 - self.h if half else self.h
        k = 1 - self.k if core else self.k
        return (h * N_Y + (self.y + dy + N_Y) % N_Y) * 2 + k

    def z_dev(self, dz):
        return (self.row_at(0, dz), self.col)

    def x_dev(self):
        return (self.row_at(1, 0), self.col)

    def y_dev(self, dy):
        return (self.row, self.col_at(0, dy, 0))

    def half_dev(self):
        return (self.row, self.col_at(1, 0, 0))

    def core_dev(self):
        return (self.row, self.col_at(0, 0, 1))

    def col_dev(self, offset):
        return (self.row, (self.col + offset) % 16)


class Wire:
    def __init__(self, send_sem, recv_sem):
        self.send_sem, self.recv_sem = send_sem, recv_sem
        self.index, self.sent = {}, []

    def slot(self, name):
        return self.index.setdefault(name, len(self.index))

    def copy(self, name, src, dst, dev):
        n = self.slot(name)
        return pltpu.make_async_remote_copy(
            src_ref=src,
            dst_ref=dst,
            send_sem=self.send_sem.at[n],
            recv_sem=self.recv_sem.at[n],
            device_id=dev,
            device_id_type=MESH,
        )

    def send(self, name, src, dst, dev):
        c = self.copy(name, src, dst, dev)
        c.start()
        self.sent.append(c)

    def arrived(self, name, landed, dev):
        self.copy(name, landed, landed, dev).wait_recv()

    def drain(self):
        for c in self.sent:
            c.wait_send()


def meet(devices):
    barrier = pltpu.get_barrier_semaphore()
    for dev in devices:
        pl.semaphore_signal(barrier, inc=1, device_id=dev, device_id_type=MESH)
    pl.semaphore_wait(barrier, len(devices))


class ColGather:
    def __init__(self, at, wire, part):
        self.at, self.wire, self.part = at, wire, part

    def peers(self):
        at = self.at
        return [at.y_dev(1), at.y_dev(-1), at.half_dev(), at.core_dev()]

    def push(self, name, col, piece, dev):
        self.wire.send(name, self.part(col, piece), self.part(col, piece), dev)

    def start(self):
        at = self.at
        self.push(("half",), at.col, None, at.half_dev())
        for d in (1, -1):
            self.push(("y", d, 1, 0), at.col, None, at.y_dev(d))
        self.push(("core", 0, 0, None), at.col, None, at.core_dev())

    def halves(self):
        at = self.at
        block = at.col_at(1, 0, 0)
        self.wire.arrived(("half",), self.part(block, None), at.half_dev())
        for d in (1, -1):
            self.push(("y", d, 1, 1), block, None, at.y_dev(d))
        self.push(("core", 1, 0, None), block, None, at.core_dev())

    def first(self, kind):
        at = self.at
        for d in (1, -1):
            block = at.col_at(kind, -d, 0)
            self.wire.arrived(("y", d, 1, kind), self.part(block, None), at.y_dev(-d))
            piece = 0 if d == 1 else 1
            self.push(("y", d, 2, kind), block, piece, at.y_dev(d))
            self.push(("core", kind, -d, None), block, None, at.core_dev())

    def second(self, kind):
        at = self.at
        for d in (1, -1):
            piece = 0 if d == 1 else 1
            block = at.col_at(kind, 2, 0)
            self.wire.arrived(("y", d, 2, kind), self.part(block, piece), at.y_dev(-d))
            self.push(("core", kind, 2, piece), block, piece, at.core_dev())

    def from_core(self):
        at = self.at
        for kind in (0, 1):
            for dy, piece in ((0, None), (-1, None), (1, None), (2, 0), (2, 1)):
                block = at.col_at(kind, dy, 1)
                self.wire.arrived(("core", kind, dy, piece), self.part(block, piece), at.core_dev())


class RowGather:
    def __init__(self, at, wire, part):
        self.at, self.wire, self.part = at, wire, part

    def peers(self):
        at = self.at
        return [at.z_dev(1), at.z_dev(-1), at.x_dev()]

    def push(self, name, row, half, piece, dev):
        self.wire.send(name, self.part(row, half, piece), self.part(row, half, piece), dev)

    def start(self):
        at = self.at
        self.push(("xa",), at.row, 0, None, at.x_dev())
        for d in (1, -1):
            for kind in (0, 1):
                self.push(("z", d, 1, kind), at.row, kind, None, at.z_dev(d))
        self.push(("xb", 0, None), at.row, 1, None, at.x_dev())

    def partner(self):
        at = self.at
        block = at.row_at(1, 0)
        self.wire.arrived(("xa",), self.part(block, 0, None), at.x_dev())
        for d in (1, -1):
            self.push(("z", d, 1, 2), block, 0, None, at.z_dev(d))

    def step(self, s, kinds=(0, 1, 2)):
        at = self.at
        for kind in kinds:
            half = 1 if kind == 1 else 0
            for d in (1, -1):
                block = at.row_at(1 if kind == 2 else 0, -d * s)
                side = 0 if d == 1 else 1
                piece = side if s == 4 else None
                self.wire.arrived(("z", d, s, kind), self.part(block, half, piece), at.z_dev(-d))
                if s < 4:
                    self.push(("z", d, s + 1, kind), block, half, side if s == 3 else None, at.z_dev(d))
                if kind == 1:
                    self.push(("xb", -d * s, piece), block, 1, piece, at.x_dev())

    def from_x(self):
        at = self.at
        for dz in (0, -1, 1, -2, 2, -3, 3, -4, 4):
            piece = {-4: 0, 4: 1}.get(dz)
            block = at.row_at(1, dz)
            self.wire.arrived(("xb", dz, piece), self.part(block, 1, piece), at.x_dev())


def row_part(ref, size):
    half_size, piece_size = size // 2, size // 4

    def part(row, half, piece):
        start = row * size + half * half_size + (0 if piece is None else piece * piece_size)
        length = half_size if piece is None else piece_size
        return ref.at[pl.ds(pl.multiple_of(start, 16), length), :]

    return part


def col_part(ref, size):
    def part(col, piece):
        start = col * size + (0 if piece is None else piece * (size // 2))
        return ref.at[pl.ds(pl.multiple_of(start, 16), size if piece is None else size // 2), :]

    return part


def project_kernel(hidden_ref, mod_ref, onehot_ref, w_ref, q_ref, k_ref, v_ref, mod_all, w_all, stats, send_sem, recv_sem):
    at = Place()
    wire = Wire(send_sem, recv_sem)
    depth, tokens = hidden_ref.shape
    rows = RowGather(at, wire, row_part(w_all, depth))
    cols = ColGather(at, wire, col_part(mod_all, depth))
    w_all[pl.ds(pl.multiple_of(at.row * depth, 16), depth), :] = w_ref[...]
    meet(rows.peers() + [at.col_dev(i) for i in range(1, 16)])
    rows.start()

    hidden = hidden_ref[...].astype(jnp.float32)
    local_mean = jnp.sum(hidden, axis=0, keepdims=True) * (1.0 / depth)
    centred = hidden - local_mean
    local_square = jnp.sum(centred * centred, axis=0, keepdims=True)
    groups = tokens // 128
    mine = stats.at[at.col]
    mine[...] = jnp.zeros(mine.shape, jnp.float32)
    for j in range(groups):
        lanes = slice(128 * j, 128 * (j + 1))
        mine[j : j + 1, :] = local_mean[:, lanes]
        mine[8 + j : 9 + j, :] = local_square[:, lanes]
    for i in range(1, 16):
        wire.send(("stat", i), stats.at[at.col], stats.at[at.col], at.col_dev(i))
    rows.partner()
    for i in range(1, 16):
        wire.arrived(("stat", i), stats.at[(at.col - i + 16) % 16], at.col_dev(16 - i))
    means, squares = stats[:, 0:8, :], stats[:, 8:16, :]
    mean = jnp.sum(means, axis=0) * (1.0 / 16)
    apart = means - mean[None]
    total = jnp.sum(squares, axis=0) + depth * jnp.sum(apart * apart, axis=0)
    inverse = lax.rsqrt(total * (1.0 / (16 * depth)) + 1e-06)

    def as_row(packed):
        return jnp.concatenate([packed[j : j + 1, :] for j in range(groups)], axis=1)

    onehot = onehot_ref[...]
    shift = jnp.dot(mod_ref[0], onehot, preferred_element_type=jnp.float32)
    scale = jnp.dot(mod_ref[1], onehot, preferred_element_type=jnp.float32)
    modulated = (hidden_ref[...].astype(jnp.float32) - as_row(mean)) * as_row(inverse) * (1.0 + scale) + shift
    mod_all[pl.ds(pl.multiple_of(at.col * depth, 16), depth), :] = modulated.astype(jnp.bfloat16)

    cols.start()
    rows.step(1)
    cols.halves()
    cols.first(0)
    rows.step(2)
    cols.first(1)
    cols.second(0)
    rows.step(3)
    cols.second(1)
    cols.from_core()
    rows.step(4)
    rows.from_x()

    width = w_ref.shape[1]

    def tile(t, carry):
        rows_at = pl.multiple_of(t * 256, 256)
        made = contract_first(mod_all[:, pl.ds(rows_at, 256)], w_all[...]).astype(jnp.bfloat16)
        for head in range(width // (3 * HD)):
            for j, ref in enumerate((q_ref, k_ref, v_ref)):
                first = (head * 3 + j) * HD
                ref[pl.ds(rows_at, 256), head * HD : (head + 1) * HD] = made[:, first : first + HD]
        return carry

    lax.fori_loop(0, tokens // 256, tile, 0)
    wire.drain()


def project(hidden_t, mod_t, onehot_t, w_qkv):
    depth, tokens = hidden_t.shape
    width = w_qkv.shape[1]
    out = jax.ShapeDtypeStruct((tokens, width // 3), jnp.bfloat16)
    vmem = pl.BlockSpec(memory_space=pltpu.VMEM)
    return pl.pallas_call(
        project_kernel,
        out_shape=(out, out, out),
        in_specs=[vmem] * 4,
        out_specs=(vmem, vmem, vmem),
        scratch_shapes=[
            pltpu.VMEM((16 * depth, tokens), jnp.bfloat16),
            pltpu.VMEM((16 * depth, width), jnp.bfloat16),
            pltpu.VMEM((16, 16, 128), jnp.float32),
            pltpu.SemaphoreType.DMA((80,)),
            pltpu.SemaphoreType.DMA((80,)),
        ],
        compiler_params=pltpu.CompilerParams(collective_id=0, has_side_effects=True, vmem_limit_bytes=VMEM_LIMIT),
        name="project",
    )(hidden_t, mod_t, onehot_t, w_qkv)


def attend_kernel(first_ref, q_ref, low_k, own_k, high_k, low_v, own_v, high_v, prefix_ref, bounds_ref, out_ref, k_all, v_all, far, score, most):
    tokens = q_ref.shape[0]
    heads = q_ref.shape[1] // HD
    groups, slot_len = prefix_ref.shape[0], prefix_ref.shape[1]
    before = groups * slot_len
    near = 3 * tokens
    base = first_ref[0]
    starts, ends, group_of = bounds_ref[0:1, :], bounds_ref[1:2, :], bounds_ref[2:3, :]
    for g in range(groups):
        at = slice(g * slot_len, (g + 1) * slot_len)
        for h in range(heads):
            k_all[at, h * HD : (h + 1) * HD] = prefix_ref[g, :, 2 * h * HD : (2 * h + 1) * HD]
            v_all[at, h * HD : (h + 1) * HD] = prefix_ref[g, :, (2 * h + 1) * HD : (2 * h + 2) * HD]
        row = jnp.where(group_of == g, 0.0, -BIG)
        far[at, :] = jnp.broadcast_to(row, (slot_len, HD)).astype(jnp.bfloat16)
    for i, (k_ref, v_ref) in enumerate(((low_k, low_v), (own_k, own_v), (high_k, high_v))):
        at = slice(before + i * tokens, before + (i + 1) * tokens)
        k_all[at, :] = k_ref[...]
        v_all[at, :] = v_ref[...]
    place = base - tokens + lax.broadcasted_iota(jnp.int32, (near, HD), 0)
    far[before:, :] = jnp.where((starts <= place) & (place < ends), 0.0, -BIG).astype(jnp.bfloat16)

    tile = 256
    block = 256
    count = (before + near) // block
    factor = math.log2(math.e) / math.sqrt(HD)

    def one_tile(t, carry):
        rows = pl.ds(pl.multiple_of(t * tile, tile), tile)
        place = base + t * tile + lax.broadcasted_iota(jnp.int32, (tile, HD), 0)
        belongs = jnp.where((starts <= place) & (place < ends), 1.0, 0.0).astype(jnp.bfloat16)
        wide = [jnp.concatenate([q_ref[rows, h * HD : (h + 1) * HD], belongs], axis=1) for h in range(heads)]
        most[...] = jnp.full(most.shape, -BIG, jnp.float32)

        def scores(b, carry):
            keys = pl.ds(pl.multiple_of(b * block, block), block)
            for h in range(heads):
                key = jnp.concatenate([k_all[keys, h * HD : (h + 1) * HD], far[keys, :]], axis=1)
                s = lax.dot_general(wide[h], key, (((1,), (1,)), ((), ())), preferred_element_type=jnp.float32)
                score[h, b] = s
                top = most[h]
                for j in range(block // HD):
                    top = jnp.maximum(top, s[:, j * HD : (j + 1) * HD])
                most[h] = top
            return carry

        lax.fori_loop(0, count, scores, 0)
        peak = [jnp.max(most[h], axis=1, keepdims=True) * factor for h in range(heads)]

        def weigh(b, carry):
            keys = pl.ds(pl.multiple_of(b * block, block), block)
            given = []
            for h in range(heads):
                mass, summed = carry[h]
                w = jnp.exp2(score[h, b] * factor - peak[h])
                for j in range(block // HD):
                    mass = mass + w[:, j * HD : (j + 1) * HD]
                summed = summed + jnp.dot(
                    w.astype(jnp.bfloat16), v_all[keys, h * HD : (h + 1) * HD], preferred_element_type=jnp.float32
                )
                given.append((mass, summed))
            return tuple(given)

        zero = jnp.zeros((tile, HD), jnp.float32)
        done = lax.fori_loop(0, count, weigh, tuple((zero, zero) for _ in range(heads)))
        for h in range(heads):
            mass, summed = done[h]
            out_ref[rows, h * HD : (h + 1) * HD] = (summed / jnp.sum(mass, axis=1, keepdims=True)).astype(jnp.bfloat16)
        return carry

    lax.fori_loop(0, tokens // tile, one_tile, 0)


def attention(first, q, keys, values, prefix, bounds):
    tokens, width = q.shape
    total = prefix.shape[0] * prefix.shape[1] + 3 * tokens
    heads = width // HD
    vmem = pl.BlockSpec(memory_space=pltpu.VMEM)
    return pl.pallas_call(
        attend_kernel,
        out_shape=jax.ShapeDtypeStruct((tokens, width), jnp.bfloat16),
        in_specs=[pl.BlockSpec(memory_space=pltpu.SMEM)] + [vmem] * 9,
        out_specs=vmem,
        scratch_shapes=[
            pltpu.VMEM((total, width), jnp.bfloat16),
            pltpu.VMEM((total, width), jnp.bfloat16),
            pltpu.VMEM((total, HD), jnp.bfloat16),
            pltpu.VMEM((heads, total // 256, 256, 256), jnp.float32),
            pltpu.VMEM((heads, 256, HD), jnp.float32),
        ],
        compiler_params=pltpu.CompilerParams(vmem_limit_bytes=VMEM_LIMIT),
        cost_estimate=pl.CostEstimate(flops=2 * tokens * total * heads * 3 * HD, bytes_accessed=8 << 20, transcendentals=tokens * total * heads),
        name="attention",
    )(first, q, *keys, *values, prefix, bounds)


def spread_kernel(block_ref, out_ref, send_sem, recv_sem):
    at = Place()
    wire = Wire(send_sem, recv_sem)
    cols = ColGather(at, wire, col_part(out_ref, block_ref.shape[0]))
    out_ref[pl.ds(pl.multiple_of(at.col * block_ref.shape[0], 16), block_ref.shape[0]), :] = block_ref[...]
    meet(cols.peers())
    cols.start()
    cols.halves()
    cols.first(0)
    cols.first(1)
    cols.second(0)
    cols.second(1)
    cols.from_core()
    wire.drain()


def spread(block):
    vmem = pl.BlockSpec(memory_space=pltpu.VMEM)
    return pl.pallas_call(
        spread_kernel,
        out_shape=jax.ShapeDtypeStruct((16 * block.shape[0], block.shape[1]), block.dtype),
        in_specs=[vmem],
        out_specs=vmem,
        scratch_shapes=[pltpu.SemaphoreType.DMA((24,)), pltpu.SemaphoreType.DMA((24,))],
        compiler_params=pltpu.CompilerParams(collective_id=1, has_side_effects=True, vmem_limit_bytes=VMEM_LIMIT),
        name="spread",
    )(block)


def shift_rows(block):
    count = lax.axis_size("row")
    up = [(i, i + 1) for i in range(count - 1)]
    down = [(i + 1, i) for i in range(count - 1)]
    return lax.ppermute(block, "row", up), lax.ppermute(block, "row", down)


def shards(hidden_in, modulation, w_qkv, w_out, prefix_cache, req_group, req_len, owner):
    tokens, features = hidden_in.shape
    requests = req_len.shape[0]
    first = lax.axis_index("row") * tokens
    slots = lax.all_gather(prefix_cache, "row", axis=0, tiled=True)
    out_weight = lax.all_gather(w_out, "row", axis=0, tiled=True)

    earlier = jnp.arange(requests)[:, None] > jnp.arange(requests)[None, :]
    starts = jnp.sum(jnp.where(earlier, req_len[None, :], 0), axis=1)
    ends = starts + req_len
    place = first + jnp.arange(tokens, dtype=jnp.int32)
    inside = (starts[:, None] <= place[None, :]) & (place[None, :] < ends[:, None])
    onehot_t = inside.astype(jnp.bfloat16)
    mod_t = jnp.transpose(modulation[:, :2], (1, 2, 0))

    q, new_keys, new_values = project(jnp.transpose(hidden_in), mod_t, onehot_t, w_qkv)

    low_k, high_k = shift_rows(new_keys)
    low_v, high_v = shift_rows(new_values)
    pad = jnp.zeros((HD - requests,), jnp.int32)
    bounds = jnp.stack([jnp.concatenate([a, pad + fill]) for a, fill in ((starts, 1 << 30), (ends, -1), (req_group, -1))])
    bounds = jnp.concatenate([bounds, jnp.zeros((5, HD), jnp.int32)])
    prefix = jnp.concatenate([lax.dynamic_slice_in_dim(slots, owner[g], 1, 0) for g in range(owner.shape[0])])
    attended = attention(
        first.reshape(1), q, (low_k, new_keys, high_k), (low_v, new_values, high_v), prefix, bounds
    )
    gathered = spread(attended)
    parts = gathered.reshape(16, tokens, attended.shape[1])
    projected = jnp.einsum(
        "jte,jef->tf", parts, out_weight.reshape(16, attended.shape[1], features), preferred_element_type=jnp.float32
    )
    gate = jnp.dot(jnp.transpose(onehot_t), modulation[:, 2], preferred_element_type=jnp.float32)
    hidden_out = (hidden_in.astype(jnp.float32) + gate * projected).astype(jnp.bfloat16)
    return hidden_out, new_keys, new_values


def solution(mesh):
    return jax.shard_map(
        shards,
        mesh=mesh,
        in_specs=(
            P("row", "col"),
            P(None, None, "col"),
            P("row", "col"),
            P("row", "col"),
            P("row", None, "col"),
            P(),
            P(),
            P(),
        ),
        out_specs=(P("row", "col"), P("row", "col"), P("row", "col")),
        check_vma=False,
    )
```

time: 499 us -> 251 us (0.50)
  waiting for transfers between devices: 313 us -> 6.32 us
  Pallas kernels: 0 us -> 188 us
  matrix products: 72.6 us -> 7.77 us
  local copies, waits for them, and re-layouts: 50.6 us -> 7.41 us
  other arithmetic: 33.2 us -> 3.94 us
  loops' own time: 10.3 us -> 0 us
  between operations: 14.4 us -> 22 us
  starting transfers between devices: 3.87 us -> 10.7 us
    all_gather x5 -> x1, waiting for transfers between devices: 310 us -> 0.01 us  [shards(): slots = lax.all_gather(prefix_cache, 'row', axis=0, tiled=True)]
    pallas_call x0 -> x3, Pallas kernels: none -> 188 us  [the longest x1 124 us: project(): pl.pallas_call(project_kernel, out_shape=(out, out, out), in_specs=[vmem]...]
    dot_general x38 -> x2, matrix products: 72.6 us -> 7.77 us  [the longest x1 6.64 us: shards(): jnp.einsum('jte,jef->tf', parts, out_weight.reshape(16, attended.shape[1]...]
    reduce_sum x39 -> x1, other arithmetic: 27.3 us -> 0.77 us  [shards(): starts = jnp.sum(jnp.where(earlier, req_len[None, :], 0), axis=1)]
    all_gather x2 -> x0, local copies, waits for them, and re-layouts: 18.4 us -> none  [the longest x1 10.7 us: shards(): lax.all_gather(hidden_in, 'col', axis=1, tiled=True)]
    dynamic_slice x32 -> x1, local copies, waits for them, and re-layouts: 17.7 us -> 1.27 us  [shards(): lax.dynamic_slice_in_dim(slots, owner[g], 1, 0)]
    another operation x1 -> x0, loops' own time: 10.3 us -> none  [shards(): running = lax.fori_loop(0, slot_block.shape[0], one_slot, running)]
    ppermute x2 -> x4, starting transfers between devices: 3.64 us -> 10.6 us  [shift_rows(): return (lax.ppermute(block, 'row', up), lax.ppermute(block, 'row', down))]
  transfers between devices with their start and end apart: 8 -> 6, of which waited for: 5 -> 2; matrix products, arithmetic and copies ran while one was open for 30% -> 4% of each run, Pallas kernels for 0% -> 76%
where the time goes in v1:
time: 251 us; the launch traced here: 246 us
  Pallas kernels  188 us (75%)
  between operations  22 us (9%)
  starting transfers between devices  10.7 us (4%)
  matrix products  7.77 us (3%)
  local copies, waits for them, and re-layouts  7.41 us (3%)
  waiting for transfers between devices  6.32 us (3%)
  other arithmetic  3.94 us (2%)
    pallas_call x1, Pallas kernels, project(): pl.pallas_call(project_kernel, out_shape=(out, out, out), in_specs=[vmem]...  124 us
    pallas_call x1, Pallas kernels, spread(): pl.pallas_call(spread_kernel, out_shape=jax.ShapeDtypeStruct((16 * block....  37.8 us
    pallas_call x1, Pallas kernels, attention(): pl.pallas_call(attend_kernel, out_shape=jax.ShapeDtypeStruct((tokens, wid...  25.8 us
    ppermute x4, starting transfers between devices, shift_rows(): return (lax.ppermute(block, 'row', up), lax.ppermute(block, 'row', down))  10.6 us
    dot_general x1, matrix products, shards(): jnp.einsum('jte,jef->tf', parts, out_weight.reshape(16, attended.shape[1]...  6.64 us
  transfers between devices with their start and end apart: 6, of which 2 were waited for; matrix products, arithmetic and copies ran while one was open for 4% of the time, Pallas kernels for 76%

profile of v1, /device:TPU:1, one launch (start us, length us, event | category | flops | bytes accessed | tf_op | source)
XLA Modules:
  0.0 245.7 jit_solution(5607940320528654988)
XLA Ops:
  7.2 0.7 all-gather.3.cloned.1.call-update
  7.9 0.7 all-gather.5.cloned.1.call-update
  8.7 0.8 select_reduce_fusion
  9.4 0.7 add.37
  10.1 0.9 slice.19
  11.0 0.8 copy.18
  11.8 0.7 fusion.15.onehot_ref
  12.5 123.9 %project.1 = (bf16[768,256]{1,0:T(8,128)(2,1)}, bf16[768,256]{1,0:T(8,128)(2,1)}, bf16[768,256]{1,0:T(8,128)(2,1)}) custom-call(bf16[320,768]{1,0:T(8,128)(2,1)} %bitcast.40, bf16[2,320,48]{2,1,0:T(8,128)(2,1)} %bitcast.39, bf16[48,768]{1,0:T(8,128)(2,1)} %fusion.15.onehot_ref, bf16[320,768]{1,0:T(8,128)(2,1)} %w_ref.1), custom_call_target="tpu_custom_call" | custom-call | tf_op jit(solution)/shard_map/project/pallas_call | solution.py:288
  136.4 1.3 collective-permute-start.1
  137.7 4.0 %collective-permute-start = (bf16[768,256]{1,0:T(8,128)(2,1)}, bf16[768,256]{1,0:T(8,128)(2,1)S(1)}, u32[]{:S(2)}, u32[]{:S(2)}) collective-permute-start(bf16[768,256]{1,0:T(8,128)(2,1)} %get-tuple-element.23.own_k), channel_id=1, source_target_pairs={{0,16},{16,32},{32,48},{48,64},{64,80},{80,96},{96,112},{112,128},... | collective-permute-start | bytes 1179656 | tf_op jit(solution)/shard_map/ppermute | solution.py:434
  141.8 1.3 collective-permute-start.3
  143.1 4.0 %collective-permute-start.2 = (bf16[768,256]{1,0:T(8,128)(2,1)}, bf16[768,256]{1,0:T(8,128)(2,1)S(1)}, u32[]{:S(2)}, u32[]{:S(2)}) collective-permute-start(bf16[768,256]{1,0:T(8,128)(2,1)} %get-tuple-element.24.own_v), channel_id=1, source_target_pairs={{0,16},{16,32},{32,48},{48,64},{64,80},{80,96},{96,112},{112,128},... | collective-permute-start | bytes 1179656 | tf_op jit(solution)/shard_map/ppermute | solution.py:434
  147.1 1.5 fusion.22
  157.1 1.1 fusion.16
  158.9 1.3 constant_dynamic-slice_fusion.3
  160.2 1.1 pad_maximum_fusion.prefix_ref
  161.3 2.9 %collective-permute-done.3.high_v = bf16[768,256]{1,0:T(8,128)(2,1)S(1)} collective-permute-done((bf16[768,256]{1,0:T(8,128)(2,1)}, bf16[768,256]{1,0:T(8,128)(2,1)S(1)}, u32[]{:S(2)}, u32[]{:S(2)}) %collective-permute-start.3) | collective-permute-done | bytes 393248 | tf_op jit(solution)/shard_map/ppermute | solution.py:434
  164.3 2.0 collective-permute-done.2.low_v
  166.3 0.7 copy-done.6
  167.0 25.8 %attention.1.block_ref = bf16[768,256]{1,0:T(8,128)(2,1)} custom-call(s32[1]{0:T(128)} %bitcast.1.first_ref, bf16[768,256]{1,0:T(8,128)(2,1)} %get-tuple-element.6.q_ref, bf16[768,256]{1,0:T(8,128)(2,1)} %copy-done.4, bf16[768,256]{1,0:T(8,128)(2,1)} %get-tuple-element.23.own_k, bf16[768,256]{1,0:T(8,128)(2,1)} %copy-done.3, bf16[768,256]{1,0:T(8,128)(2,1)} %copy-done.6, ...), custom_call_target="tpu_custom_call" | custom-call | flops 3925868544 | bytes 8388608 | tf_op jit(solution)/shard_map/attention/pallas_call | solution.py:383
  192.8 37.8 %spread.1 = bf16[12288,256]{1,0:T(8,128)(2,1)} custom-call(bf16[768,256]{1,0:T(8,128)(2,1)} %attention.1.block_ref), custom_call_target="tpu_custom_call" | custom-call | tf_op jit(solution)/shard_map/spread/pallas_call | solution.py:419
  230.8 6.6 %fusion.12 = bf16[768,320]{0,1:T(8,128)(2,1)} fusion(f32[768,320]{0,1:T(8,128)S(1)} %fusion.16, bf16[16,768,256]{2,1,0:T(8,128)(2,1)} %bitcast.38, bf16[40,16,8,256]{3,2,1,0:T(8,128)(2,1)} %bitcast.41, bf16[768,320]{0,1:T(8,128)(2,1)S(1)} %copy-done), kind=kOutput, calls=%fused_computation.6 | convolution fusion | flops 2014248960 | bytes 10878976 | tf_op jit(solution)/shard_map/jte,jef->tf/dot_general | solution.py:465
  237.4 0.7 copy.34
  238.2 0.7 copy.35
  (25 shorter events, 1.5 us)
Async XLA Ops:
  7.2 151.8 %all-gather.3.cloned.1.call-start = ((), (), s32[]{:S(2)}) async-start(), calls=%async_computation | async-start | bytes 4456448 | tf_op jit(solution)/shard_map/all_gather | solution.py:441
  7.9 222.8 %all-gather.5.cloned.1.call-start = ((), (), s32[]{:S(2)}) async-start(), calls=%async_computation.1 | async-start | bytes 2785280 | tf_op jit(solution)/shard_map/all_gather | solution.py:442
  136.4 24.9 %collective-permute-start.1 = (bf16[768,256]{1,0:T(8,128)(2,1)}, bf16[768,256]{1,0:T(8,128)(2,1)S(1)}, u32[]{:S(2)}, u32[]{:S(2)}) collective-permute-start(bf16[768,256]{1,0:T(8,128)(2,1)} %get-tuple-element.23.own_k), channel_id=1, source_target_pairs={{16,0},{32,16},{48,32},{64,48},{80,64},{96,80},{112,96},{128,112},... | collective-permute-start | bytes 1179656 | tf_op jit(solution)/shard_map/ppermute | solution.py:434
  137.7 23.6 %collective-permute-start = (bf16[768,256]{1,0:T(8,128)(2,1)}, bf16[768,256]{1,0:T(8,128)(2,1)S(1)}, u32[]{:S(2)}, u32[]{:S(2)}) collective-permute-start(bf16[768,256]{1,0:T(8,128)(2,1)} %get-tuple-element.23.own_k), channel_id=1, source_target_pairs={{0,16},{16,32},{32,48},{48,64},{64,80},{80,96},{96,112},{112,128},... | collective-permute-start | bytes 1179656 | tf_op jit(solution)/shard_map/ppermute | solution.py:434
  141.8 22.5 %collective-permute-start.3 = (bf16[768,256]{1,0:T(8,128)(2,1)}, bf16[768,256]{1,0:T(8,128)(2,1)S(1)}, u32[]{:S(2)}, u32[]{:S(2)}) collective-permute-start(bf16[768,256]{1,0:T(8,128)(2,1)} %get-tuple-element.24.own_v), channel_id=1, source_target_pairs={{16,0},{32,16},{48,32},{64,48},{80,64},{96,80},{112,96},{128,112},... | collective-permute-start | bytes 1179656 | tf_op jit(solution)/shard_map/ppermute | solution.py:434
  143.1 23.2 %collective-permute-start.2 = (bf16[768,256]{1,0:T(8,128)(2,1)}, bf16[768,256]{1,0:T(8,128)(2,1)S(1)}, u32[]{:S(2)}, u32[]{:S(2)}) collective-permute-start(bf16[768,256]{1,0:T(8,128)(2,1)} %get-tuple-element.24.own_v), channel_id=1, source_target_pairs={{0,16},{16,32},{32,48},{48,64},{64,80},{80,96},{96,112},{112,128},... | collective-permute-start | bytes 1179656 | tf_op jit(solution)/shard_map/ppermute | solution.py:434
  161.3 4.9 %copy-start.3 = (bf16[768,256]{1,0:T(8,128)(2,1)}, bf16[768,256]{1,0:T(8,128)(2,1)S(1)}, u32[]{:S(2)}) copy-start(bf16[768,256]{1,0:T(8,128)(2,1)S(1)} %collective-permute-done.1.high_k) | copy-start | bytes 1179652
  161.3 4.9 %copy-start.4 = (bf16[768,256]{1,0:T(8,128)(2,1)}, bf16[768,256]{1,0:T(8,128)(2,1)S(1)}, u32[]{:S(2)}) copy-start(bf16[768,256]{1,0:T(8,128)(2,1)S(1)} %collective-permute-done.low_k) | copy-start | bytes 1179652
  164.3 2.0 copy-start.5
  166.3 0.7 copy-start.6
  192.8 37.9 %copy-start = (bf16[768,320]{0,1:T(8,128)(2,1)S(1)}, bf16[768,320]{0,1:T(8,128)(2,1)}, u32[]{:S(2)}) copy-start(bf16[768,320]{0,1:T(8,128)(2,1)} %param.8) | copy-start | bytes 1474564
  230.7 6.7 %copy-start.2 = (bf16[768,256]{1,0:T(8,128)(2,1)S(1)}, bf16[768,256]{1,0:T(8,128)(2,1)}, u32[]{:S(2)}) copy-start(bf16[768,256]{1,0:T(8,128)(2,1)} %get-tuple-element.23.own_k) | copy-start | bytes 1179652
  230.7 7.4 %copy-start.1 = (bf16[768,256]{1,0:T(8,128)(2,1)S(1)}, bf16[768,256]{1,0:T(8,128)(2,1)}, u32[]{:S(2)}) copy-start(bf16[768,256]{1,0:T(8,128)(2,1)} %get-tuple-element.24.own_v) | copy-start | bytes 1179652
Sparse Core Ops, SparseCore 0:
  9.8 105.1 all-gather.2
  116.7 73.0 all-gather.4

commit v2 on v1

v2 whole, which is shorter than its diff:
```python
import functools
import math

import jax
import jax.numpy as jnp
from jax import lax
from jax.experimental import pallas as pl
from jax.experimental.pallas import tpu as pltpu
from jax.sharding import PartitionSpec as P

HD = 128
N_Z = 8
N_Y = 4
MESH = pl.DeviceIdType.MESH
BIG = 1e30
HALO = 672
VMEM_LIMIT = 56 << 20


def contract_first(a, b):
    return lax.dot_general(a, b, (((0,), (0,)), ((), ())), preferred_element_type=jnp.float32)


class Place:
    def __init__(self):
        self.row, self.col = lax.axis_index("row"), lax.axis_index("col")
        self.l, self.z = self.row // N_Z, self.row % N_Z
        self.h, self.y, self.k = self.col // (2 * N_Y), (self.col // 2) % N_Y, self.col % 2

    def row_at(self, plane, dz):
        l = 1 - self.l if plane else self.l
        return l * N_Z + (self.z + dz + N_Z) % N_Z

    def col_at(self, half, dy, core):
        h = 1 - self.h if half else self.h
        k = 1 - self.k if core else self.k
        return (h * N_Y + (self.y + dy + N_Y) % N_Y) * 2 + k

    def z_dev(self, dz):
        return (self.row_at(0, dz), self.col)

    def x_dev(self):
        return (self.row_at(1, 0), self.col)

    def y_dev(self, dy):
        return (self.row, self.col_at(0, dy, 0))

    def half_dev(self):
        return (self.row, self.col_at(1, 0, 0))

    def core_dev(self):
        return (self.row, self.col_at(0, 0, 1))

    def col_dev(self, offset):
        return (self.row, (self.col + offset) % 16)


class Wire:
    def __init__(self, send_sem, recv_sem):
        self.send_sem, self.recv_sem = send_sem, recv_sem
        self.index, self.sent = {}, []

    def slot(self, name):
        return self.index.setdefault(name, len(self.index))

    def copy(self, name, src, dst, dev):
        n = self.slot(name)
        return pltpu.make_async_remote_copy(
            src_ref=src,
            dst_ref=dst,
            send_sem=self.send_sem.at[n],
            recv_sem=self.recv_sem.at[n],
            device_id=dev,
            device_id_type=MESH,
        )

    def send(self, name, src, dst, dev):
        c = self.copy(name, src, dst, dev)
        c.start()
        self.sent.append(c)

    def arrived(self, name, landed, dev):
        self.copy(name, landed, landed, dev).wait_recv()

    def drain(self):
        for c in self.sent:
            c.wait_send()


def meet(devices):
    barrier = pltpu.get_barrier_semaphore()
    for dev in devices:
        pl.semaphore_signal(barrier, inc=1, device_id=dev, device_id_type=MESH)
    pl.semaphore_wait(barrier, len(devices))


class ColGather:
    def __init__(self, at, wire, part):
        self.at, self.wire, self.part = at, wire, part

    def peers(self):
        at = self.at
        return [at.y_dev(1), at.y_dev(-1), at.half_dev(), at.core_dev()]

    def push(self, name, col, piece, dev):
        self.wire.send(name, self.part(col, piece), self.part(col, piece), dev)

    def start(self):
        at = self.at
        self.push(("half",), at.col, None, at.half_dev())
        for d in (1, -1):
            self.push(("y", d, 1, 0), at.col, None, at.y_dev(d))
        self.push(("core", 0, 0, None), at.col, None, at.core_dev())

    def halves(self):
        at = self.at
        block = at.col_at(1, 0, 0)
        self.wire.arrived(("half",), self.part(block, None), at.half_dev())
        for d in (1, -1):
            self.push(("y", d, 1, 1), block, None, at.y_dev(d))
        self.push(("core", 1, 0, None), block, None, at.core_dev())

    def first(self, kind):
        at = self.at
        for d in (1, -1):
            block = at.col_at(kind, -d, 0)
            self.wire.arrived(("y", d, 1, kind), self.part(block, None), at.y_dev(-d))
            piece = 0 if d == 1 else 1
            self.push(("y", d, 2, kind), block, piece, at.y_dev(d))
            self.push(("core", kind, -d, None), block, None, at.core_dev())

    def second(self, kind):
        at = self.at
        for d in (1, -1):
            piece = 0 if d == 1 else 1
            block = at.col_at(kind, 2, 0)
            self.wire.arrived(("y", d, 2, kind), self.part(block, piece), at.y_dev(-d))
            self.push(("core", kind, 2, piece), block, piece, at.core_dev())

    def from_core(self, blocks):
        at = self.at
        for kind, dy in blocks:
            for piece in (0, 1) if dy == 2 else (None,):
                block = at.col_at(kind, dy, 1)
                self.wire.arrived(("core", kind, dy, piece), self.part(block, piece), at.core_dev())


class RowGather:
    def __init__(self, at, wire, part, tag):
        self.at, self.wire, self.part, self.tag = at, wire, part, tag

    def peers(self):
        at = self.at
        return [at.z_dev(1), at.z_dev(-1), at.x_dev()]

    def push(self, name, row, half, piece, dev):
        self.wire.send((self.tag,) + name, self.part(row, half, piece), self.part(row, half, piece), dev)

    def land(self, name, row, half, piece, dev):
        self.wire.arrived((self.tag,) + name, self.part(row, half, piece), dev)

    def start(self):
        at = self.at
        self.push(("xa",), at.row, 0, None, at.x_dev())
        for d in (1, -1):
            for kind in (0, 1):
                self.push(("z", d, 1, kind), at.row, kind, None, at.z_dev(d))
        self.push(("xb", 0, None), at.row, 1, None, at.x_dev())

    def partner(self):
        at = self.at
        block = at.row_at(1, 0)
        self.land(("xa",), block, 0, None, at.x_dev())
        for d in (1, -1):
            self.push(("z", d, 1, 2), block, 0, None, at.z_dev(d))

    def step(self, s, kinds=(0, 1, 2)):
        at = self.at
        for kind in kinds:
            half = 1 if kind == 1 else 0
            for d in (1, -1):
                block = at.row_at(1 if kind == 2 else 0, -d * s)
                side = 0 if d == 1 else 1
                piece = side if s == 4 else None
                self.land(("z", d, s, kind), block, half, piece, at.z_dev(-d))
                if s < 4:
                    self.push(("z", d, s + 1, kind), block, half, side if s == 3 else None, at.z_dev(d))
                if kind == 1:
                    self.push(("xb", -d * s, piece), block, 1, piece, at.x_dev())

    def from_x(self, offsets=(0, -1, 1, -2, 2, -3, 3, -4, 4)):
        at = self.at
        for dz in offsets:
            piece = {-4: 0, 4: 1}.get(dz)
            self.land(("xb", dz, piece), at.row_at(1, dz), 1, piece, at.x_dev())


def row_part(ref, size):
    half_size, piece_size = size // 2, size // 4

    def part(row, half, piece):
        start = row * size + half * half_size + (0 if piece is None else piece * piece_size)
        length = half_size if piece is None else piece_size
        return ref.at[pl.ds(pl.multiple_of(start, 16), length), :]

    return part


def col_part(ref, size):
    def part(col, piece):
        start = col * size + (0 if piece is None else piece * (size // 2))
        return ref.at[pl.ds(pl.multiple_of(start, 16), size if piece is None else size // 2), :]

    return part


def project_kernel(
    owner_ref, hidden_ref, mod_ref, onehot_ref, w_ref, slot_ref, q_ref, k_ref, v_ref, near_ref, prefix_ref,
    mod_all, w_all, acc, stats, pieces, send_sem, recv_sem,
):
    at = Place()
    wire = Wire(send_sem, recv_sem)
    depth, tokens = hidden_ref.shape
    width = w_ref.shape[1]
    groups = owner_ref.shape[0]
    piece = slot_ref.shape[0] // 16
    rows = RowGather(at, wire, row_part(w_all, depth), "w")
    shared = RowGather(at, wire, row_part(prefix_ref, groups * piece), "p")
    cols = ColGather(at, wire, col_part(mod_all, depth))
    row_devs = [((at.row + i) % 16, at.col) for i in range(16)]
    w_all[pl.ds(pl.multiple_of(at.row * depth, 16), depth), :] = w_ref[...]
    meet(row_devs[1:] + [at.col_dev(i) for i in range(1, 16)])
    rows.start()

    hidden = hidden_ref[...].astype(jnp.float32)
    local_mean = jnp.sum(hidden, axis=0, keepdims=True) * (1.0 / depth)
    centred = hidden - local_mean
    local_square = jnp.sum(centred * centred, axis=0, keepdims=True)
    spans = tokens // 128
    mine = stats.at[at.col]
    mine[...] = jnp.zeros(mine.shape, jnp.float32)
    for j in range(spans):
        lanes = slice(128 * j, 128 * (j + 1))
        mine[j : j + 1, :] = local_mean[:, lanes]
        mine[8 + j : 9 + j, :] = local_square[:, lanes]
    for i in range(1, 16):
        wire.send(("stat", i), stats.at[at.col], stats.at[at.col], at.col_dev(i))

    def piece_at(ref, index):
        return ref.at[pl.ds(pl.multiple_of(index * piece, 16), piece), :]

    for i in range(1, 16):
        wire.send(("slot", i), piece_at(slot_ref, (at.row + i) % 16), piece_at(pieces, at.row), row_devs[i])
    piece_at(pieces, at.row)[...] = piece_at(slot_ref, at.row)[...]
    rows.partner()
    for i in range(1, 16):
        wire.arrived(("stat", i), stats.at[(at.col - i + 16) % 16], at.col_dev(16 - i))
    means, squares = stats[:, 0:8, :], stats[:, 8:16, :]
    mean = jnp.sum(means, axis=0) * (1.0 / 16)
    apart = means - mean[None]
    total = jnp.sum(squares, axis=0) + depth * jnp.sum(apart * apart, axis=0)
    inverse = lax.rsqrt(total * (1.0 / (16 * depth)) + 1e-06)

    def as_row(packed):
        return jnp.concatenate([packed[j : j + 1, :] for j in range(spans)], axis=1)

    onehot = onehot_ref[...]
    shift = jnp.dot(mod_ref[0], onehot, preferred_element_type=jnp.float32)
    scale = jnp.dot(mod_ref[1], onehot, preferred_element_type=jnp.float32)
    modulated = (hidden_ref[...].astype(jnp.float32) - as_row(mean)) * as_row(inverse) * (1.0 + scale) + shift
    mod_all[pl.ds(pl.multiple_of(at.col * depth, 16), depth), :] = modulated.astype(jnp.bfloat16)
    cols.start()

    for i in range(1, 16):
        wire.arrived(("slot", i), piece_at(pieces, (at.row + 16 - i) % 16), row_devs[16 - i])
    from_slot = lax.broadcasted_iota(jnp.int32, (piece, 16 * piece), 1)
    own_line = lax.broadcasted_iota(jnp.int32, (piece, 16 * piece), 0)
    for g in range(groups):
        picks = jnp.where(from_slot == owner_ref[g] * piece + own_line, 1.0, 0.0).astype(jnp.bfloat16)
        chosen = jnp.dot(picks, pieces[...], preferred_element_type=jnp.float32).astype(jnp.bfloat16)
        prefix_ref[pl.ds(pl.multiple_of((at.row * groups + g) * piece, 16), piece), :] = chosen
    shared.start()

    def product(blocks, tile):
        starts = [pl.multiple_of(at.row_at(plane, dz) * depth, 16) for plane, dz in blocks]
        lanes = pl.ds(pl.multiple_of(tile * 256, 256), 256)
        left = jnp.concatenate([mod_all[pl.ds(s, depth), lanes] for s in starts], axis=0)
        right = jnp.concatenate([w_all[pl.ds(s, depth), :] for s in starts], axis=0)
        return contract_first(left, right)

    def accumulate(blocks, fresh=False):
        def one(tile, carry):
            at_rows = pl.ds(pl.multiple_of(tile * 256, 256), 256)
            made = product(blocks, tile)
            acc[at_rows, :] = made if fresh else acc[at_rows, :] + made
            return carry

        lax.fori_loop(0, tokens // 256, one, 0)

    rows.step(1)
    cols.halves()
    cols.first(0)
    shared.partner()
    rows.step(2)
    cols.first(1)
    cols.second(0)
    shared.step(1)
    rows.step(3)
    cols.second(1)
    cols.from_core([(kind, dy) for kind in (0, 1) for dy in (0, -1, 1, 2)])
    shared.step(2)
    accumulate([(0, 0), (0, -1), (0, 1), (0, -2)], True)
    rows.step(4)
    shared.step(3)
    rows.from_x((0,))
    accumulate([(0, 2), (0, -3), (0, 3), (1, 0)])
    rows.from_x((-1, 1, -2, 2))
    accumulate([(1, -1), (1, 1), (1, -2), (1, 2)])
    shared.step(4)
    rows.from_x((-3, 3, -4, 4))

    heads = width // (3 * HD)
    near = near_ref.shape[0]
    own = (near - tokens) // 2
    ahead, behind = ((at.row + 1) % 16, at.col), ((at.row + 15) % 16, at.col)
    edge = own - HALO
    near_ref[0:edge, :] = jnp.zeros((edge, near_ref.shape[1]), jnp.bfloat16)
    near_ref[near - edge : near, :] = jnp.zeros((edge, near_ref.shape[1]), jnp.bfloat16)
    spans_ahead, spans_behind = [], []
    for tile in range(tokens // 256):
        low, high = tile * 256, (tile + 1) * 256
        made = (acc[low:high, :] + product([(0, 4), (1, -3), (1, 3), (1, 4)], tile)).astype(jnp.bfloat16)
        for head in range(heads):
            first = head * 3 * HD
            lanes = slice(head * HD, (head + 1) * HD)
            q_ref[low:high, lanes] = made[:, first : first + HD]
            k_ref[low:high, lanes] = made[:, first + HD : first + 2 * HD]
            v_ref[low:high, lanes] = made[:, first + 2 * HD : first + 3 * HD]
            near_ref[own + low : own + high, 2 * head * HD : 2 * (head + 1) * HD] = made[:, first + HD : first + 3 * HD]
        begin = max(low, tokens - HALO)
        spans_ahead.append((begin, high))
        wire.send(("up", tile), near_ref.at[own + begin : own + high, :], near_ref.at[begin - tokens + own : high - tokens + own, :], ahead)
        finish = min(high, HALO)
        spans_behind.append((low, finish))
        wire.send(("down", tile), near_ref.at[own + low : own + finish, :], near_ref.at[own + tokens + low : own + tokens + finish, :], behind)
    shared.from_x()
    for tile, (begin, high) in enumerate(spans_ahead):
        wire.arrived(("up", tile), near_ref.at[begin - tokens + own : high - tokens + own, :], behind)
    for tile, (low, finish) in enumerate(spans_behind):
        wire.arrived(("down", tile), near_ref.at[own + tokens + low : own + tokens + finish, :], ahead)
    wire.drain()


def project(owner, hidden_t, mod_t, onehot_t, w_qkv, slot):
    depth, tokens = hidden_t.shape
    width = w_qkv.shape[1]
    groups, slot_len = owner.shape[0], slot.shape[0]
    heads = width // (3 * HD)

    def out(rows, columns):
        return jax.ShapeDtypeStruct((rows, columns), jnp.bfloat16)

    own = out(tokens, heads * HD)
    vmem = pl.BlockSpec(memory_space=pltpu.VMEM)
    return pl.pallas_call(
        project_kernel,
        out_shape=(own, own, own, out(3 * tokens, 2 * heads * HD), out(groups * slot_len, 2 * heads * HD)),
        in_specs=[pl.BlockSpec(memory_space=pltpu.SMEM)] + [vmem] * 5,
        out_specs=(vmem,) * 5,
        scratch_shapes=[
            pltpu.VMEM((16 * depth, tokens), jnp.bfloat16),
            pltpu.VMEM((16 * depth, width), jnp.bfloat16),
            pltpu.VMEM((tokens, width), jnp.float32),
            pltpu.VMEM((16, 16, 128), jnp.float32),
            pltpu.VMEM((slot_len, 2 * heads * HD), jnp.bfloat16),
            pltpu.SemaphoreType.DMA((128,)),
            pltpu.SemaphoreType.DMA((128,)),
        ],
        compiler_params=pltpu.CompilerParams(collective_id=0, has_side_effects=True, vmem_limit_bytes=VMEM_LIMIT),
        name="project",
    )(owner, hidden_t, mod_t, onehot_t, w_qkv, slot)


def attend_kernel(first_ref, len_ref, group_ref, q_ref, near_ref, prefix_ref, bounds_ref, out_ref, far, score, most, blocks):
    tokens = q_ref.shape[0]
    heads = q_ref.shape[1] // HD
    requests = len_ref.shape[0]
    holders, groups, piece, _ = prefix_ref.shape
    base = first_ref[0]
    starts, ends, group_of = bounds_ref[0:1, :], bounds_ref[1:2, :], bounds_ref[2:3, :]
    near = near_ref.shape[0]
    own = (near - tokens) // 2
    tile = 256; block = 256
    factor = math.log2(math.e) / math.sqrt(HD)
    place = base - own + lax.broadcasted_iota(jnp.int32, (near, HD), 0)
    far[...] = jnp.where((starts <= place) & (place < ends), 0.0, -BIG).astype(jnp.bfloat16)

    def one_tile(t, carry):
        top_pos = base + t * tile
        def scan(r, c):
            start, low, high, f = c
            end = start + len_ref[r]
            hit = (start < top_pos + tile) & (end > top_pos)
            g = group_ref[r]
            low = jnp.where(hit, jnp.minimum(low, start), low)
            high = jnp.where(hit, jnp.maximum(high, end), high)
            f = tuple(jnp.where(hit & (g == i), 1, f[i]) for i in range(groups))
            return end, low, high, f
        _, low, high, flags = lax.fori_loop(0, requests, scan, (jnp.int32(0), top_pos, top_pos, (jnp.int32(0),) * groups))
        low_block = (low - (base - own)) // block
        high_block = (high - (base - own) + block - 1) // block
        rows = pl.ds(pl.multiple_of(t * tile, tile), tile)
        place = top_pos + lax.broadcasted_iota(jnp.int32, (tile, HD), 0)
        belongs = jnp.where((starts <= place) & (place < ends), 1.0, 0.0).astype(jnp.bfloat16)
        wide = [jnp.concatenate([q_ref[rows, h * HD : (h + 1) * HD], belongs], axis=1) for h in range(heads)]
        most[...] = jnp.full(most.shape, -BIG, jnp.float32)

        def score_block(n, keys_of, mask):
            for h in range(heads):
                key = jnp.concatenate([keys_of(h), mask], axis=1)
                s = lax.dot_general(wide[h], key, (((1,), (1,)), ((), ())), preferred_element_type=jnp.float32)
                score[h, n] = s
                top = most[h]
                for j in range(block // HD):
                    top = jnp.maximum(top, s[:, j * HD : (j + 1) * HD])
                most[h] = top

        def group_part(g, j):
            return prefix_ref[:, g, :, j * HD : (j + 1) * HD].reshape(block, HD)

        used = jnp.int32(0)
        for g in range(groups):
            @pl.when(flags[g] > 0)
            def _():
                mask = jnp.broadcast_to(jnp.where(group_of == g, 0.0, -BIG), (block, HD)).astype(jnp.bfloat16)
                score_block(g, lambda h: group_part(g, 2 * h), mask)

        def near_scores(b, c):
            keys = pl.ds(pl.multiple_of(b * block, block), block)
            score_block(groups + b, lambda h: near_ref[keys, 2 * h * HD : (2 * h + 1) * HD], far[keys, :])
            return c
        lax.fori_loop(low_block, high_block, near_scores, 0)
        peak = [jnp.max(most[h], axis=1, keepdims=True) * factor for h in range(heads)]
        most[...] = jnp.zeros(most.shape, jnp.float32)
        blocks[...] = jnp.zeros(blocks.shape, jnp.float32)

        def weigh(n, values_of):
            for h in range(heads):
                w = jnp.exp2(score[h, n] * factor - peak[h])
                mass = most[h]
                for j in range(block // HD):
                    mass = mass + w[:, j * HD : (j + 1) * HD]
                most[h] = mass
                blocks[h] += jnp.dot(w.astype(jnp.bfloat16), values_of(h), preferred_element_type=jnp.float32)

        for g in range(groups):
            @pl.when(flags[g] > 0)
            def _():
                weigh(g, lambda h: group_part(g, 2 * h + 1))

        def near_weigh(b, c):
            keys = pl.ds(pl.multiple_of(b * block, block), block)
            weigh(groups + b, lambda h: near_ref[keys, (2 * h + 1) * HD : (2 * h + 2) * HD])
            return c
        lax.fori_loop(low_block, high_block, near_weigh, 0)
        for h in range(heads):
            out_ref[rows, h * HD : (h + 1) * HD] = (blocks[h] / jnp.sum(most[h], axis=1, keepdims=True)).astype(jnp.bfloat16)
        return carry
    lax.fori_loop(0, tokens // tile, one_tile, 0)

def attention(first, req_len, req_group, q, near, prefix, bounds):
    tokens, width = q.shape
    heads = width // HD
    total = near.shape[0]
    tile = 256
    vmem = pl.BlockSpec(memory_space=pltpu.VMEM)
    return pl.pallas_call(
        attend_kernel,
        out_shape=jax.ShapeDtypeStruct((tokens, width), jnp.bfloat16),
        in_specs=[pl.BlockSpec(memory_space=pltpu.SMEM)]*3 + [vmem] * 4,
        out_specs=vmem,
        scratch_shapes=[
            pltpu.VMEM((total, HD), jnp.bfloat16),
            pltpu.VMEM((heads, prefix.shape[1] + total // 256, tile, 256), jnp.float32),
            pltpu.VMEM((heads, tile, HD), jnp.float32),
            pltpu.VMEM((heads, tile, HD), jnp.float32),
        ],
        compiler_params=pltpu.CompilerParams(vmem_limit_bytes=VMEM_LIMIT),
        name="attention",
    )(first, req_len, req_group, q, near, prefix, bounds)


def output_kernel(
    block_ref, w_ref, hidden_ref, onehot_ref, gate_ref, out_ref, att_all, w_all, acc, send_sem, recv_sem
):
    at = Place()
    wire = Wire(send_sem, recv_sem)
    tokens = block_ref.shape[0]
    features = w_ref.shape[0]
    cols = ColGather(at, wire, col_part(att_all, tokens))
    rows = RowGather(at, wire, row_part(w_all, features), "w")
    meet(rows.peers() + cols.peers())
    att_all[pl.ds(pl.multiple_of(at.col * tokens, 16), tokens), :] = block_ref[...]
    cols.start()
    w_all[pl.ds(pl.multiple_of(at.row * features, 16), features), :] = w_ref[...]
    rows.start()
    gate = contract_first(onehot_ref[...], gate_ref[...])

    def accumulate(blocks, fresh=False):
        indices = [at.col_at(kind, dy, core) for kind, dy, core in blocks]
        right = jnp.concatenate([w_all[pl.ds(pl.multiple_of(i * features, 16), features), :] for i in indices], axis=1)

        def one(tile, carry):
            left = jnp.concatenate(
                [att_all[pl.ds(pl.multiple_of(i * tokens + tile * 256, 16), 256), :] for i in indices], axis=1
            )
            made = lax.dot_general(left, right, (((1,), (1,)), ((), ())), preferred_element_type=jnp.float32)
            at_rows = pl.ds(pl.multiple_of(tile * 256, 256), 256)
            acc[at_rows, :] = made if fresh else acc[at_rows, :] + made
            return carry

        lax.fori_loop(0, tokens // 256, one, 0)

    rows.partner()
    cols.halves()
    rows.step(1)
    rows.step(2)
    cols.first(0)
    rows.step(3)
    cols.first(1)
    rows.step(4)
    rows.from_x()
    cols.from_core([(0, 0), (1, 0)])
    accumulate([(0, 0, 0), (1, 0, 0), (0, 0, 1), (1, 0, 1)], True)
    cols.second(0)
    cols.second(1)
    accumulate([(0, -1, 0), (0, 1, 0), (1, -1, 0), (1, 1, 0)])
    cols.from_core([(0, -1), (0, 1), (1, -1), (1, 1)])
    accumulate([(0, -1, 1), (0, 1, 1), (1, -1, 1), (1, 1, 1)])
    cols.from_core([(0, 2), (1, 2)])
    accumulate([(0, 2, 0), (0, 2, 1), (1, 2, 0), (1, 2, 1)])
    out_ref[...] = (hidden_ref[...].astype(jnp.float32) + gate * acc[...]).astype(jnp.bfloat16)
    wire.drain()


def output(attended, w_t, hidden, onehot_t, gate):
    tokens, width = attended.shape
    features = w_t.shape[0]
    vmem = pl.BlockSpec(memory_space=pltpu.VMEM)
    return pl.pallas_call(
        output_kernel,
        out_shape=jax.ShapeDtypeStruct(hidden.shape, jnp.bfloat16),
        in_specs=[vmem] * 5,
        out_specs=vmem,
        scratch_shapes=[
            pltpu.VMEM((16 * tokens, width), jnp.bfloat16),
            pltpu.VMEM((16 * features, width), jnp.bfloat16),
            pltpu.VMEM((tokens, features), jnp.float32),
            pltpu.SemaphoreType.DMA((64,)),
            pltpu.SemaphoreType.DMA((64,)),
        ],
        compiler_params=pltpu.CompilerParams(collective_id=1, has_side_effects=True, vmem_limit_bytes=VMEM_LIMIT),
        name="output",
    )(attended, w_t, hidden, onehot_t, gate)


def shards(hidden_in, modulation, w_qkv, w_out, prefix_cache, req_group, req_len, owner):
    tokens, features = hidden_in.shape
    requests = req_len.shape[0]
    groups, slot_len = owner.shape[0], prefix_cache.shape[1]
    first = lax.axis_index("row") * tokens
    earlier = jnp.arange(requests)[:, None] > jnp.arange(requests)[None, :]
    starts = jnp.sum(jnp.where(earlier, req_len[None, :], 0), axis=1)
    ends = starts + req_len
    place = first + jnp.arange(tokens, dtype=jnp.int32)
    inside = (starts[:, None] <= place[None, :]) & (place[None, :] < ends[:, None])
    onehot_t = inside.astype(jnp.bfloat16)
    mod_t = jnp.transpose(modulation[:, :2], (1, 2, 0))
    q, new_keys, new_values, near, prefix = project(
        owner, jnp.transpose(hidden_in), mod_t, onehot_t, w_qkv, prefix_cache[0]
    )
    pad = jnp.zeros((HD - requests,), jnp.int32)
    bounds = jnp.stack([jnp.concatenate([a, pad + fill]) for a, fill in ((starts, 1 << 30), (ends, -1), (req_group, -1))])
    bounds = jnp.concatenate([bounds, jnp.zeros((5, HD), jnp.int32)])
    prefix = prefix.reshape(16, groups, slot_len // 16, prefix.shape[1])
    attended = attention(first.reshape(1), req_len, req_group, q, near, prefix, bounds)
    hidden_out = output(attended, jnp.transpose(w_out), hidden_in, onehot_t, modulation[:, 2])
    return hidden_out, new_keys, new_values


def solution(mesh):
    return jax.shard_map(
        shards,
        mesh=mesh,
        in_specs=(
            P("row", "col"),
            P(None, None, "col"),
            P("row", "col"),
            P("row", "col"),
            P("row", None, "col"),
            P(),
            P(),
            P(),
        ),
        out_specs=(P("row", "col"), P("row", "col"), P("row", "col")),
        check_vma=False,
    )
```

time: 251 us -> 179 us (0.71); the launches traced: 246 us -> 178 us
  Pallas kernels: 188 us -> 166 us
  between operations: 22 us -> 0.67 us
  starting transfers between devices: 10.7 us -> 0 us
  matrix products: 7.77 us -> 0 us
  waiting for transfers between devices: 6.32 us -> 0 us
    pallas_call x1, Pallas kernels: 25.8 us -> 11.8 us  [attention(): pl.pallas_call(attend_kernel, out_shape=jax.ShapeDtypeStruct((tokens, wid...]
    ppermute x4 -> x0, starting transfers between devices: 10.6 us -> none  [shift_rows(): return (lax.ppermute(block, 'row', up), lax.ppermute(block, 'row', down))]
    dot_general x2 -> x0, matrix products: 7.77 us -> none  [the longest x1 6.64 us: shards(): jnp.einsum('jte,jef->tf', parts, out_weight.reshape(16, attended.shape[1]...]
    pallas_call x2, Pallas kernels: 162 us -> 154 us  [the longest x1 107 us: project(): pl.pallas_call(project_kernel, out_shape=(own, own, own, out(3 * tokens,...]
    ppermute x4 -> x0, waiting for transfers between devices: 4.92 us -> none  [shift_rows(): return (lax.ppermute(block, 'row', up), lax.ppermute(block, 'row', down))]
    unnamed x17 -> x11, local copies, waits for them, and re-layouts: 3.06 us -> 5.43 us
  transfers between devices with their start and end apart: 6 -> 0, of which waited for: 2 -> 0; matrix products, arithmetic and copies ran while one was open for 4% -> 0% of each run, Pallas kernels for 76% -> 0%
where the time goes in v2:
time: 179 us; the launch traced here: 178 us
  Pallas kernels  166 us (93%)
  local copies, waits for them, and re-layouts  8.51 us (5%)
  other arithmetic  2.83 us (2%)
    pallas_call x1, Pallas kernels, project(): pl.pallas_call(project_kernel, out_shape=(own, own, own, out(3 * tokens,...  107 us
    pallas_call x1, Pallas kernels, output(): pl.pallas_call(output_kernel, out_shape=jax.ShapeDtypeStruct(hidden.shape...  47 us
    pallas_call x1, Pallas kernels, attention(): pl.pallas_call(attend_kernel, out_shape=jax.ShapeDtypeStruct((tokens, wid...  11.8 us
    unnamed x11, local copies, waits for them, and re-layouts  5.43 us

profile of v2, /device:TPU:1, one launch (start us, length us, event | category | flops | bytes accessed | tf_op | source)
XLA Modules:
  0.0 178.3 jit_solution(9387944812904050576)
XLA Ops:
  0.6 0.8 select_reduce_fusion
  1.4 0.7 add.22
  2.1 0.7 and_convert_fusion.onehot_ref
  2.8 0.9 slice.6
  3.7 0.8 copy.17
  4.5 107.5 %project.1 = (bf16[768,256]{1,0:T(8,128)(2,1)}, bf16[768,256]{1,0:T(8,128)(2,1)}, bf16[768,256]{1,0:T(8,128)(2,1)}, bf16[2304,512]{1,0:T(8,128)(2,1)}, bf16[1024,512]{1,0:T(8,128)(2,1)}) custom-call(s32[4]{0:T(128)} %owner_ref.1, bf16[320,768]{1,0:T(8,128)(2,1)} %bitcast.14, bf16[2,320,48]{2,1,0:T(8,128)(2,1)} %bitcast.16, ...), custom_call_target="tpu_custom_call" | custom-call | tf_op jit(solution)/shard_map/project/pallas_call | solution.py:365
  112.0 0.0 copy-start
  112.0 0.7 pad_bitcast_fusion
  112.7 0.1 pad.6.clone
  112.8 0.7 add_add_fusion.bounds_ref
  113.5 11.8 %attention.1.block_ref = bf16[768,256]{1,0:T(8,128)(2,1)} custom-call(s32[1]{0:T(128)} %bitcast.first_ref, s32[48]{0:T(128)} %len_ref.1, s32[48]{0:T(128)} %group_ref.1, bf16[768,256]{1,0:T(8,128)(2,1)} %get-tuple-element.8.q_ref, bf16[2304,512]{1,0:T(8,128)(2,1)} %get-tuple-element.9.near_ref, bf16[16,4,16,512]{3,2,1,0:T(8,128)(2,1)} %bitcast.15, ...), custom_call_target="tpu_custom_call" | custom-call | tf_op jit(solution)/shard_map/attention/pallas_call | solution.py:477
  125.3 0.0 copy-done
  125.3 0.0 copy-start.2
  125.3 0.0 copy-start.1
  125.3 1.1 copy.15.hidden_ref
  126.4 1.4 slice_bitcast_fusion.gate_ref
  127.8 47.0 %output.1 = bf16[768,320]{1,0:T(8,128)(2,1)} custom-call(bf16[768,256]{1,0:T(8,128)(2,1)} %attention.1.block_ref, bf16[320,256]{1,0:T(8,128)(2,1)} %bitcast.18, bf16[768,320]{1,0:T(8,128)(2,1)} %copy.15.hidden_ref, bf16[48,768]{1,0:T(8,128)(2,1)} %and_convert_fusion.onehot_ref, bf16[48,320]{1,0:T(8,128)(2,1)} %slice_bitcast_fusion.gate_ref), custom_call_target="tpu_custom_call" | custom-call | tf_op jit(solution)/shard_map/output/pallas_call | solution.py:550
  174.7 2.1 %copy.16 = bf16[768,320]{0,1:T(8,128)(2,1)} copy(bf16[768,320]{1,0:T(8,128)(2,1)} %output.1) | data formatting | bytes 983040
  176.8 0.0 copy-done.2
  176.8 0.7 copy.20
  177.6 0.0 copy-done.1
  177.6 0.7 copy.21
  (3 shorter events, 0.0 us)
Async XLA Ops:
  112.0 13.3 %copy-start = (bf16[768,320]{0,1:T(8,128)(2,1)S(1)}, bf16[768,320]{0,1:T(8,128)(2,1)}, u32[]{:S(2)}) copy-start(bf16[768,320]{0,1:T(8,128)(2,1)} %param.8) | copy-start | bytes 1474564
  125.3 51.5 %copy-start.2 = (bf16[768,256]{1,0:T(8,128)(2,1)S(1)}, bf16[768,256]{1,0:T(8,128)(2,1)}, u32[]{:S(2)}) copy-start(bf16[768,256]{1,0:T(8,128)(2,1)} %get-tuple-element.25) | copy-start | bytes 1179652
  125.3 52.2 %copy-start.1 = (bf16[768,256]{1,0:T(8,128)(2,1)S(1)}, bf16[768,256]{1,0:T(8,128)(2,1)}, u32[]{:S(2)}) copy-start(bf16[768,256]{1,0:T(8,128)(2,1)} %get-tuple-element.26) | copy-start | bytes 1179652

commit v3 on v2

--- a/solution.py
+++ b/solution.py
@@ -1,4 +1,3 @@
-import functools
 import math
 
 import jax
@@ -14,7 +13,8 @@
 MESH = pl.DeviceIdType.MESH
 BIG = 1e30
 HALO = 672
-VMEM_LIMIT = 56 << 20
+VMEM_LIMIT = 60 << 20
+TILE = 256
 
 
 def contract_first(a, b):
@@ -95,15 +95,18 @@
 
 
 class ColGather:
-    def __init__(self, at, wire, part):
-        self.at, self.wire, self.part = at, wire, part
+    def __init__(self, at, wire, part, tag):
+        self.at, self.wire, self.part, self.tag = at, wire, part, tag
 
     def peers(self):
         at = self.at
         return [at.y_dev(1), at.y_dev(-1), at.half_dev(), at.core_dev()]
 
     def push(self, name, col, piece, dev):
-        self.wire.send(name, self.part(col, piece), self.part(col, piece), dev)
+        self.wire.send((self.tag,) + name, self.part(col, piece), self.part(col, piece), dev)
+
+    def land(self, name, col, piece, dev):
+        self.wire.arrived((self.tag,) + name, self.part(col, piece), dev)
 
     def start(self):
         at = self.at
@@ -115,7 +118,7 @@
     def halves(self):
         at = self.at
         block = at.col_at(1, 0, 0)
-        self.wire.arrived(("half",), self.part(block, None), at.half_dev())
+        self.land(("half",), block, None, at.half_dev())
         for d in (1, -1):
             self.push(("y", d, 1, 1), block, None, at.y_dev(d))
         self.push(("core", 1, 0, None), block, None, at.core_dev())
@@ -124,9 +127,8 @@
         at = self.at
         for d in (1, -1):
             block = at.col_at(kind, -d, 0)
-            self.wire.arrived(("y", d, 1, kind), self.part(block, None), at.y_dev(-d))
-            piece = 0 if d == 1 else 1
-            self.push(("y", d, 2, kind), block, piece, at.y_dev(d))
+            self.land(("y", d, 1, kind), block, None, at.y_dev(-d))
+            self.push(("y", d, 2, kind), block, 0 if d == 1 else 1, at.y_dev(d))
             self.push(("core", kind, -d, None), block, None, at.core_dev())
 
     def second(self, kind):
@@ -134,15 +136,14 @@
         for d in (1, -1):
             piece = 0 if d == 1 else 1
             block = at.col_at(kind, 2, 0)
-            self.wire.arrived(("y", d, 2, kind), self.part(block, piece), at.y_dev(-d))
+            self.land(("y", d, 2, kind), block, piece, at.y_dev(-d))
             self.push(("core", kind, 2, piece), block, piece, at.core_dev())
 
-    def from_core(self, blocks):
-        at = self.at
-        for kind, dy in blocks:
+    def from_core(self):
+        at = self.at
+        for kind, dy in ((0, 0), (1, 0), (0, -1), (0, 1), (1, -1), (1, 1), (0, 2), (1, 2)):
             for piece in (0, 1) if dy == 2 else (None,):
-                block = at.col_at(kind, dy, 1)
-                self.wire.arrived(("core", kind, dy, piece), self.part(block, piece), at.core_dev())
+                self.land(("core", kind, dy, piece), at.col_at(kind, dy, 1), piece, at.core_dev())
 
 
 class RowGather:
@@ -195,23 +196,57 @@
             self.land(("xb", dz, piece), at.row_at(1, dz), 1, piece, at.x_dev())
 
 
-def row_part(ref, size):
-    half_size, piece_size = size // 2, size // 4
-
+def row_part(ref, size, crossing):
     def part(row, half, piece):
-        start = row * size + half * half_size + (0 if piece is None else piece * piece_size)
-        length = half_size if piece is None else piece_size
+        length = size - crossing if half else crossing
+        start = row * size + half * crossing
+        if piece is not None:
+            length = length // 2
+            start = start + piece * length
         return ref.at[pl.ds(pl.multiple_of(start, 16), length), :]
 
     return part
 
 
-def col_part(ref, size):
+def col_part(ref, size, offset=0, length=None):
+    length = size if length is None else length
+
     def part(col, piece):
-        start = col * size + (0 if piece is None else piece * (size // 2))
-        return ref.at[pl.ds(pl.multiple_of(start, 16), size if piece is None else size // 2), :]
+        start = col * size + offset + (0 if piece is None else piece * (length // 2))
+        return ref.at[pl.ds(pl.multiple_of(start, 16), length if piece is None else length // 2), :]
 
     return part
+
+
+def request_bounds(len_ref, group_ref, base, tokens):
+    requests = len_ref.shape[0]
+    line = lax.broadcasted_iota(jnp.int32, (requests, HD), 0)
+    lane = lax.broadcasted_iota(jnp.int32, (8, HD), 1)
+
+    def bound(r, carry):
+        start, start_col, end_col, start_row, end_row, group_row = carry
+        end = start + len_ref[r]
+        here, there = line == r, lane == r
+        return (
+            end,
+            jnp.where(here, start, start_col),
+            jnp.where(here, end, end_col),
+            jnp.where(there, start, start_row),
+            jnp.where(there, end, end_row),
+            jnp.where(there, group_ref[r], group_row),
+        )
+
+    column = jnp.zeros((requests, HD), jnp.int32)
+    flat = jnp.full((8, HD), -1, jnp.int32)
+    _, start_col, end_col, start_row, end_row, group_row = lax.fori_loop(
+        0, requests, bound, (jnp.int32(0), column, column, flat, flat, flat)
+    )
+    start_row, end_row, group_row = start_row[0:1], end_row[0:1], group_row[0:1]
+    place = base + lax.broadcasted_iota(jnp.int32, (requests, tokens), 1)
+    begins = jnp.concatenate([start_col] * (tokens // HD), axis=1)
+    ends = jnp.concatenate([end_col] * (tokens // HD), axis=1)
+    onehot = jnp.where((begins <= place) & (place < ends), 1.0, 0.0).astype(jnp.bfloat16)
+    return start_row, end_row, group_row, onehot
 
 
 def project_kernel(
@@ -224,9 +259,9 @@
     width = w_ref.shape[1]
     groups = owner_ref.shape[0]
     piece = slot_ref.shape[0] // 16
-    rows = RowGather(at, wire, row_part(w_all, depth), "w")
-    shared = RowGather(at, wire, row_part(prefix_ref, groups * piece), "p")
-    cols = ColGather(at, wire, col_part(mod_all, depth))
+    rows = RowGather(at, wire, row_part(w_all, depth, 128), "w")
+    shared = RowGather(at, wire, row_part(prefix_ref, groups * piece, groups * piece // 2), "p")
+    cols = ColGather(at, wire, col_part(mod_all, depth), "m")
     row_devs = [((at.row + i) % 16, at.col) for i in range(16)]
     w_all[pl.ds(pl.multiple_of(at.row * depth, 16), depth), :] = w_ref[...]
     meet(row_devs[1:] + [at.col_dev(i) for i in range(1, 16)])
@@ -307,7 +342,7 @@
     shared.step(1)
     rows.step(3)
     cols.second(1)
-    cols.from_core([(kind, dy) for kind in (0, 1) for dy in (0, -1, 1, 2)])
+    cols.from_core()
     shared.step(2)
     accumulate([(0, 0), (0, -1), (0, 1), (0, -2)], True)
     rows.step(4)
@@ -381,193 +416,126 @@
     )(owner, hidden_t, mod_t, onehot_t, w_qkv, slot)
 
 
-def attend_kernel(first_ref, len_ref, group_ref, q_ref, near_ref, prefix_ref, bounds_ref, out_ref, far, score, most, blocks):
-    tokens = q_ref.shape[0]
-    heads = q_ref.shape[1] // HD
-    requests = len_ref.shape[0]
-    holders, groups, piece, _ = prefix_ref.shape
-    base = first_ref[0]
-    starts, ends, group_of = bounds_ref[0:1, :], bounds_ref[1:2, :], bounds_ref[2:3, :]
-    near = near_ref.shape[0]
-    own = (near - tokens) // 2
-    tile = 256; block = 256
+def attend_kernel(
+    len_ref, group_ref, mod_ref, w_out_ref, hidden_ref, q_all, near, prefix, out_ref,
+    far, far_prefix, att_all, w_out_all, send_sem, recv_sem,
+):
+    at = Place()
+    wire = Wire(send_sem, recv_sem)
+    tokens = q_all.shape[0]
+    heads = q_all.shape[1] // HD
+    features = w_out_ref.shape[0]
+    tiles = tokens // TILE
+    groups = 4
+    piece = prefix.shape[0] // (16 * groups)
+    weights = RowGather(at, wire, row_part(w_out_all, features, features // 2), "o")
+    outs = [ColGather(at, wire, col_part(att_all, tokens, t * TILE, TILE), ("a", t)) for t in range(tiles)]
+
+    def span(start, length):
+        return pl.ds(pl.multiple_of(start, 16), length)
+
+    w_out_all[span(at.row * features, features), :] = w_out_ref[...]
+    meet(weights.peers() + outs[0].peers())
+    weights.start()
+    base = at.row * tokens
+    start_row, end_row, group_row, onehot = request_bounds(len_ref, group_ref, base, tokens)
+    near_len = near.shape[0]
+    own = (near_len - tokens) // 2
+    spot = base - own + lax.broadcasted_iota(jnp.int32, (near_len, HD), 0)
+    far[...] = jnp.where((start_row <= spot) & (spot < end_row), 0.0, -BIG).astype(jnp.bfloat16)
+    held = [jnp.broadcast_to(jnp.where(group_row == g, 0.0, -BIG), (piece, HD)) for g in range(groups)]
+    held = jnp.concatenate(held, axis=0).astype(jnp.bfloat16)
+    for r in range(16):
+        far_prefix[r * groups * piece : (r + 1) * groups * piece, :] = held
+    weights.partner()
     factor = math.log2(math.e) / math.sqrt(HD)
-    place = base - own + lax.broadcasted_iota(jnp.int32, (near, HD), 0)
-    far[...] = jnp.where((starts <= place) & (place < ends), 0.0, -BIG).astype(jnp.bfloat16)
-
-    def one_tile(t, carry):
-        top_pos = base + t * tile
-        def scan(r, c):
-            start, low, high, f = c
-            end = start + len_ref[r]
-            hit = (start < top_pos + tile) & (end > top_pos)
-            g = group_ref[r]
-            low = jnp.where(hit, jnp.minimum(low, start), low)
-            high = jnp.where(hit, jnp.maximum(high, end), high)
-            f = tuple(jnp.where(hit & (g == i), 1, f[i]) for i in range(groups))
-            return end, low, high, f
-        _, low, high, flags = lax.fori_loop(0, requests, scan, (jnp.int32(0), top_pos, top_pos, (jnp.int32(0),) * groups))
-        low_block = (low - (base - own)) // block
-        high_block = (high - (base - own) + block - 1) // block
-        rows = pl.ds(pl.multiple_of(t * tile, tile), tile)
-        place = top_pos + lax.broadcasted_iota(jnp.int32, (tile, HD), 0)
-        belongs = jnp.where((starts <= place) & (place < ends), 1.0, 0.0).astype(jnp.bfloat16)
-        wide = [jnp.concatenate([q_ref[rows, h * HD : (h + 1) * HD], belongs], axis=1) for h in range(heads)]
-        most[...] = jnp.full(most.shape, -BIG, jnp.float32)
-
-        def score_block(n, keys_of, mask):
-            for h in range(heads):
-                key = jnp.concatenate([keys_of(h), mask], axis=1)
-                s = lax.dot_general(wide[h], key, (((1,), (1,)), ((), ())), preferred_element_type=jnp.float32)
-                score[h, n] = s
-                top = most[h]
-                for j in range(block // HD):
-                    top = jnp.maximum(top, s[:, j * HD : (j + 1) * HD])
-                most[h] = top
-
-        def group_part(g, j):
-            return prefix_ref[:, g, :, j * HD : (j + 1) * HD].reshape(block, HD)
-
-        used = jnp.int32(0)
-        for g in range(groups):
-            @pl.when(flags[g] > 0)
-            def _():
-                mask = jnp.broadcast_to(jnp.where(group_of == g, 0.0, -BIG), (block, HD)).astype(jnp.bfloat16)
-                score_block(g, lambda h: group_part(g, 2 * h), mask)
-
-        def near_scores(b, c):
-            keys = pl.ds(pl.multiple_of(b * block, block), block)
-            score_block(groups + b, lambda h: near_ref[keys, 2 * h * HD : (2 * h + 1) * HD], far[keys, :])
-            return c
-        lax.fori_loop(low_block, high_block, near_scores, 0)
-        peak = [jnp.max(most[h], axis=1, keepdims=True) * factor for h in range(heads)]
-        most[...] = jnp.zeros(most.shape, jnp.float32)
-        blocks[...] = jnp.zeros(blocks.shape, jnp.float32)
-
-        def weigh(n, values_of):
-            for h in range(heads):
-                w = jnp.exp2(score[h, n] * factor - peak[h])
-                mass = most[h]
-                for j in range(block // HD):
-                    mass = mass + w[:, j * HD : (j + 1) * HD]
-                most[h] = mass
-                blocks[h] += jnp.dot(w.astype(jnp.bfloat16), values_of(h), preferred_element_type=jnp.float32)
-
-        for g in range(groups):
-            @pl.when(flags[g] > 0)
-            def _():
-                weigh(g, lambda h: group_part(g, 2 * h + 1))
-
-        def near_weigh(b, c):
-            keys = pl.ds(pl.multiple_of(b * block, block), block)
-            weigh(groups + b, lambda h: near_ref[keys, (2 * h + 1) * HD : (2 * h + 2) * HD])
-            return c
-        lax.fori_loop(low_block, high_block, near_weigh, 0)
+    window = TILE + 2 * (HALO + 32)
+
+    def attend(t):
+        place = base + t * TILE + lax.broadcasted_iota(jnp.int32, (TILE, HD), 0)
+        belongs = jnp.where((start_row <= place) & (place < end_row), 1.0, 0.0).astype(jnp.bfloat16)
+        seen = slice(own + t * TILE - HALO - 32, own + t * TILE - HALO - 32 + window)
+        made = []
+        hidden_from = jnp.concatenate([far_prefix[...], far[seen, :]], axis=0)
         for h in range(heads):
-            out_ref[rows, h * HD : (h + 1) * HD] = (blocks[h] / jnp.sum(most[h], axis=1, keepdims=True)).astype(jnp.bfloat16)
-        return carry
-    lax.fori_loop(0, tokens // tile, one_tile, 0)
-
-def attention(first, req_len, req_group, q, near, prefix, bounds):
-    tokens, width = q.shape
-    heads = width // HD
-    total = near.shape[0]
-    tile = 256
+            lanes = slice(h * HD, (h + 1) * HD)
+            of_key, of_value = slice(2 * h * HD, (2 * h + 1) * HD), slice((2 * h + 1) * HD, (2 * h + 2) * HD)
+            query = jnp.concatenate([q_all[t * TILE : (t + 1) * TILE, lanes], belongs], axis=1)
+            key = jnp.concatenate([jnp.concatenate([prefix[:, of_key], near[seen, of_key]], axis=0), hidden_from], axis=1)
+            score = lax.dot_general(query, key, (((1,), (1,)), ((), ())), preferred_element_type=jnp.float32)
+            peak = jnp.max(score, axis=1, keepdims=True) * factor
+            weight = jnp.exp2(score * factor - peak)
+            mass = jnp.sum(weight, axis=1, keepdims=True)
+            value = jnp.concatenate([prefix[:, of_value], near[seen, of_value]], axis=0)
+            summed = jnp.dot(weight.astype(jnp.bfloat16), value, preferred_element_type=jnp.float32)
+            made.append((summed / mass).astype(jnp.bfloat16))
+        att_all[span(at.col * tokens + t * TILE, TILE), :] = jnp.concatenate(made, axis=1)
+        outs[t].start()
+
+    attend(0)
+    weights.step(1)
+    attend(1)
+    outs[0].halves()
+    outs[0].first(0)
+    weights.step(2)
+    attend(2)
+    outs[0].first(1)
+    outs[1].halves()
+    outs[1].first(0)
+    weights.step(3)
+    outs[0].second(0)
+    outs[1].first(1)
+    outs[2].halves()
+    outs[0].second(1)
+    outs[2].first(0)
+    weights.step(4)
+    outs[1].second(0)
+    outs[2].first(1)
+    outs[1].second(1)
+    weights.from_x()
+    gate = contract_first(onehot, mod_ref[2])
+    right = jnp.concatenate([w_out_all[j * features : (j + 1) * features, :] for j in range(16)], axis=1)
+
+    def finish_tile(t):
+        low, high = t * TILE, (t + 1) * TILE
+        outs[t].from_core()
+        left = jnp.concatenate([att_all[j * tokens + low : j * tokens + high, :] for j in range(16)], axis=1)
+        made = lax.dot_general(left, right, (((1,), (1,)), ((), ())), preferred_element_type=jnp.float32)
+        out_ref[low:high, :] = (hidden_ref[low:high, :].astype(jnp.float32) + gate[low:high, :] * made).astype(jnp.bfloat16)
+
+    finish_tile(0)
+    outs[2].second(0)
+    outs[2].second(1)
+    finish_tile(1)
+    finish_tile(2)
+    wire.drain()
+
+
+def attend(req_len, req_group, mod, w_out_t, hidden, q, near, prefix):
+    tokens, own = q.shape
+    features = hidden.shape[1]
     vmem = pl.BlockSpec(memory_space=pltpu.VMEM)
     return pl.pallas_call(
         attend_kernel,
-        out_shape=jax.ShapeDtypeStruct((tokens, width), jnp.bfloat16),
-        in_specs=[pl.BlockSpec(memory_space=pltpu.SMEM)]*3 + [vmem] * 4,
+        out_shape=jax.ShapeDtypeStruct(hidden.shape, jnp.bfloat16),
+        in_specs=[pl.BlockSpec(memory_space=pltpu.SMEM)] * 2 + [vmem] * 6,
         out_specs=vmem,
         scratch_shapes=[
-            pltpu.VMEM((total, HD), jnp.bfloat16),
-            pltpu.VMEM((heads, prefix.shape[1] + total // 256, tile, 256), jnp.float32),
-            pltpu.VMEM((heads, tile, HD), jnp.float32),
-            pltpu.VMEM((heads, tile, HD), jnp.float32),
-        ],
-        compiler_params=pltpu.CompilerParams(vmem_limit_bytes=VMEM_LIMIT),
-        name="attention",
-    )(first, req_len, req_group, q, near, prefix, bounds)
-
-
-def output_kernel(
-    block_ref, w_ref, hidden_ref, onehot_ref, gate_ref, out_ref, att_all, w_all, acc, send_sem, recv_sem
-):
-    at = Place()
-    wire = Wire(send_sem, recv_sem)
-    tokens = block_ref.shape[0]
-    features = w_ref.shape[0]
-    cols = ColGather(at, wire, col_part(att_all, tokens))
-    rows = RowGather(at, wire, row_part(w_all, features), "w")
-    meet(rows.peers() + cols.peers())
-    att_all[pl.ds(pl.multiple_of(at.col * tokens, 16), tokens), :] = block_ref[...]
-    cols.start()
-    w_all[pl.ds(pl.multiple_of(at.row * features, 16), features), :] = w_ref[...]
-    rows.start()
-    gate = contract_first(onehot_ref[...], gate_ref[...])
-
-    def accumulate(blocks, fresh=False):
-        indices = [at.col_at(kind, dy, core) for kind, dy, core in blocks]
-        right = jnp.concatenate([w_all[pl.ds(pl.multiple_of(i * features, 16), features), :] for i in indices], axis=1)
-
-        def one(tile, carry):
-            left = jnp.concatenate(
-                [att_all[pl.ds(pl.multiple_of(i * tokens + tile * 256, 16), 256), :] for i in indices], axis=1
-            )
-            made = lax.dot_general(left, right, (((1,), (1,)), ((), ())), preferred_element_type=jnp.float32)
-            at_rows = pl.ds(pl.multiple_of(tile * 256, 256), 256)
-            acc[at_rows, :] = made if fresh else acc[at_rows, :] + made
-            return carry
-
-        lax.fori_loop(0, tokens // 256, one, 0)
-
-    rows.partner()
-    cols.halves()
-    rows.step(1)
-    rows.step(2)
-    cols.first(0)
-    rows.step(3)
-    cols.first(1)
-    rows.step(4)
-    rows.from_x()
-    cols.from_core([(0, 0), (1, 0)])
-    accumulate([(0, 0, 0), (1, 0, 0), (0, 0, 1), (1, 0, 1)], True)
-    cols.second(0)
-    cols.second(1)
-    accumulate([(0, -1, 0), (0, 1, 0), (1, -1, 0), (1, 1, 0)])
-    cols.from_core([(0, -1), (0, 1), (1, -1), (1, 1)])
-    accumulate([(0, -1, 1), (0, 1, 1), (1, -1, 1), (1, 1, 1)])
-    cols.from_core([(0, 2), (1, 2)])
-    accumulate([(0, 2, 0), (0, 2, 1), (1, 2, 0), (1, 2, 1)])
-    out_ref[...] = (hidden_ref[...].astype(jnp.float32) + gate * acc[...]).astype(jnp.bfloat16)
-    wire.drain()
-
-
-def output(attended, w_t, hidden, onehot_t, gate):
-    tokens, width = attended.shape
-    features = w_t.shape[0]
-    vmem = pl.BlockSpec(memory_space=pltpu.VMEM)
-    return pl.pallas_call(
-        output_kernel,
-        out_shape=jax.ShapeDtypeStruct(hidden.shape, jnp.bfloat16),
-        in_specs=[vmem] * 5,
-        out_specs=vmem,
-        scratch_shapes=[
-            pltpu.VMEM((16 * tokens, width), jnp.bfloat16),
-            pltpu.VMEM((16 * features, width), jnp.bfloat16),
-            pltpu.VMEM((tokens, features), jnp.float32),
-            pltpu.SemaphoreType.DMA((64,)),
-            pltpu.SemaphoreType.DMA((64,)),
+            pltpu.VMEM((near.shape[0], HD), jnp.bfloat16),
+            pltpu.VMEM((prefix.shape[0], HD), jnp.bfloat16),
+            pltpu.VMEM((16 * tokens, own), jnp.bfloat16),
+            pltpu.VMEM((16 * features, own), jnp.bfloat16),
+            pltpu.SemaphoreType.DMA((96,)),
+            pltpu.SemaphoreType.DMA((96,)),
         ],
         compiler_params=pltpu.CompilerParams(collective_id=1, has_side_effects=True, vmem_limit_bytes=VMEM_LIMIT),
-        name="output",
-    )(attended, w_t, hidden, onehot_t, gate)
+        name="attend",
+    )(req_len, req_group, mod, w_out_t, hidden, q, near, prefix)
 
 
 def shards(hidden_in, modulation, w_qkv, w_out, prefix_cache, req_group, req_len, owner):
-    tokens, features = hidden_in.shape
+    tokens = hidden_in.shape[0]
     requests = req_len.shape[0]
-    groups, slot_len = owner.shape[0], prefix_cache.shape[1]
     first = lax.axis_index("row") * tokens
     earlier = jnp.arange(requests)[:, None] > jnp.arange(requests)[None, :]
     starts = jnp.sum(jnp.where(earlier, req_len[None, :], 0), axis=1)
@@ -579,12 +547,8 @@
     q, new_keys, new_values, near, prefix = project(
         owner, jnp.transpose(hidden_in), mod_t, onehot_t, w_qkv, prefix_cache[0]
     )
-    pad = jnp.zeros((HD - requests,), jnp.int32)
-    bounds = jnp.stack([jnp.concatenate([a, pad + fill]) for a, fill in ((starts, 1 << 30), (ends, -1), (req_group, -1))])
-    bounds = jnp.concatenate([bounds, jnp.zeros((5, HD), jnp.int32)])
-    prefix = prefix.reshape(16, groups, slot_len // 16, prefix.shape[1])
-    attended = attention(first.reshape(1), req_len, req_group, q, near, prefix, bounds)
-    hidden_out = output(attended, jnp.transpose(w_out), hidden_in, onehot_t, modulation[:, 2])
+    mod = jnp.transpose(modulation, (1, 0, 2))
+    hidden_out = attend(req_len, req_group, mod, jnp.transpose(w_out), hidden_in, q, near, prefix)
     return hidden_out, new_keys, new_values
 
 

time: 179 us -> 169 us (0.944)
  Pallas kernels: 166 us -> 158 us
    pallas_call x2 -> x1, Pallas kernels: 58.8 us -> 47.5 us  [attend(): pl.pallas_call(attend_kernel, out_shape=jax.ShapeDtypeStruct(hidden.shape...]
    pallas_call x1, Pallas kernels: 107 us -> 111 us  [project(): pl.pallas_call(project_kernel, out_shape=(own, own, own, out(3 * tokens,...]
    unnamed x11 -> x9, local copies, waits for them, and re-layouts: 5.43 us -> 6.46 us
where the time goes in v3:
time: 169 us
  Pallas kernels  158 us (93%)
  local copies, waits for them, and re-layouts  7.35 us (4%)
  other arithmetic  2.16 us (1%)
    pallas_call x1, Pallas kernels, project(): pl.pallas_call(project_kernel, out_shape=(own, own, own, out(3 * tokens,...  111 us
    pallas_call x1, Pallas kernels, attend(): pl.pallas_call(attend_kernel, out_shape=jax.ShapeDtypeStruct(hidden.shape...  47.5 us
    unnamed x9, local copies, waits for them, and re-layouts  6.46 us

profile of v3, /device:TPU:1, one launch (start us, length us, event | category | flops | bytes accessed | tf_op | source)
XLA Modules:
  0.0 168.7 jit_solution(1513122217481676857)
XLA Ops:
  0.6 0.8 select_reduce_fusion
  1.4 0.7 add.15
  2.1 0.7 and_convert_fusion.onehot_ref
  2.8 0.9 slice.3
  3.7 0.8 copy.17
  4.5 2.1 %copy.15.hidden_ref = bf16[768,320]{1,0:T(8,128)(2,1)} copy(bf16[768,320]{0,1:T(8,128)(2,1)} %param.8) | data formatting | bytes 983040 | tf_op args[0]
  6.6 110.9 %project.1 = (bf16[768,256]{1,0:T(8,128)(2,1)}, bf16[768,256]{1,0:T(8,128)(2,1)}, bf16[768,256]{1,0:T(8,128)(2,1)}, bf16[2304,512]{1,0:T(8,128)(2,1)}, bf16[1024,512]{1,0:T(8,128)(2,1)}) custom-call(s32[4]{0:T(128)} %owner_ref.1, bf16[320,768]{1,0:T(8,128)(2,1)} %bitcast.5, bf16[2,320,48]{2,1,0:T(8,128)(2,1)} %bitcast.6, ...), custom_call_target="tpu_custom_call" | custom-call | tf_op jit(solution)/shard_map/project/pallas_call | solution.py:400
  117.5 0.0 copy-start.1
  117.5 0.0 copy-start
  117.5 47.5 %attend.1 = bf16[768,320]{1,0:T(8,128)(2,1)} custom-call(s32[48]{0:T(128)} %len_ref.1, s32[48]{0:T(128)} %group_ref.1, bf16[3,48,320]{2,1,0:T(8,128)(2,1)} %bitcast.7, bf16[320,256]{1,0:T(8,128)(2,1)} %bitcast.9, bf16[768,320]{1,0:T(8,128)(2,1)} %copy.15.hidden_ref, bf16[768,256]{1,0:T(8,128)(2,1)} %get-tuple-element.8.q_all, ...), custom_call_target="tpu_custom_call" | custom-call | tf_op jit(solution)/shard_map/attend/pallas_call | solution.py:518
  165.1 2.1 %copy.16 = bf16[768,320]{0,1:T(8,128)(2,1)} copy(bf16[768,320]{1,0:T(8,128)(2,1)} %attend.1) | data formatting | bytes 983040
  167.2 0.0 copy-done.1
  167.2 0.7 copy.20
  167.9 0.0 copy-done
  167.9 0.7 copy.21
  (1 shorter events, 0.0 us)
Async XLA Ops:
  117.5 49.6 %copy-start.1 = (bf16[768,256]{1,0:T(8,128)(2,1)S(1)}, bf16[768,256]{1,0:T(8,128)(2,1)}, u32[]{:S(2)}) copy-start(bf16[768,256]{1,0:T(8,128)(2,1)} %get-tuple-element.23) | copy-start | bytes 1179652
  117.5 50.4 %copy-start = (bf16[768,256]{1,0:T(8,128)(2,1)S(1)}, bf16[768,256]{1,0:T(8,128)(2,1)}, u32[]{:S(2)}) copy-start(bf16[768,256]{1,0:T(8,128)(2,1)} %get-tuple-element.24) | copy-start | bytes 1179652

commit v4 on v3

--- a/solution.py
+++ b/solution.py
@@ -87,11 +87,14 @@
             c.wait_send()
 
 
-def meet(devices):
+def greet(devices):
     barrier = pltpu.get_barrier_semaphore()
     for dev in devices:
         pl.semaphore_signal(barrier, inc=1, device_id=dev, device_id_type=MESH)
-    pl.semaphore_wait(barrier, len(devices))
+
+
+def meet(devices):
+    pl.semaphore_wait(pltpu.get_barrier_semaphore(), len(devices))
 
 
 class ColGather:
@@ -263,9 +266,9 @@
     shared = RowGather(at, wire, row_part(prefix_ref, groups * piece, groups * piece // 2), "p")
     cols = ColGather(at, wire, col_part(mod_all, depth), "m")
     row_devs = [((at.row + i) % 16, at.col) for i in range(16)]
+    met = row_devs[1:] + [at.col_dev(i) for i in range(1, 16)]
+    greet(met)
     w_all[pl.ds(pl.multiple_of(at.row * depth, 16), depth), :] = w_ref[...]
-    meet(row_devs[1:] + [at.col_dev(i) for i in range(1, 16)])
-    rows.start()
 
     hidden = hidden_ref[...].astype(jnp.float32)
     local_mean = jnp.sum(hidden, axis=0, keepdims=True) * (1.0 / depth)
@@ -278,8 +281,10 @@
         lanes = slice(128 * j, 128 * (j + 1))
         mine[j : j + 1, :] = local_mean[:, lanes]
         mine[8 + j : 9 + j, :] = local_square[:, lanes]
+    meet(met)
     for i in range(1, 16):
         wire.send(("stat", i), stats.at[at.col], stats.at[at.col], at.col_dev(i))
+    rows.start()
 
     def piece_at(ref, index):
         return ref.at[pl.ds(pl.multiple_of(index * piece, 16), piece), :]
@@ -435,8 +440,8 @@
         return pl.ds(pl.multiple_of(start, 16), length)
 
     w_out_all[span(at.row * features, features), :] = w_out_ref[...]
-    meet(weights.peers() + outs[0].peers())
-    weights.start()
+    met = weights.peers() + outs[0].peers()
+    greet(met)
     base = at.row * tokens
     start_row, end_row, group_row, onehot = request_bounds(len_ref, group_ref, base, tokens)
     near_len = near.shape[0]
@@ -447,7 +452,6 @@
     held = jnp.concatenate(held, axis=0).astype(jnp.bfloat16)
     for r in range(16):
         far_prefix[r * groups * piece : (r + 1) * groups * piece, :] = held
-    weights.partner()
     factor = math.log2(math.e) / math.sqrt(HD)
     window = TILE + 2 * (HALO + 32)
 
@@ -470,15 +474,20 @@
             summed = jnp.dot(weight.astype(jnp.bfloat16), value, preferred_element_type=jnp.float32)
             made.append((summed / mass).astype(jnp.bfloat16))
         att_all[span(at.col * tokens + t * TILE, TILE), :] = jnp.concatenate(made, axis=1)
-        outs[t].start()
 
     attend(0)
+    meet(met)
+    outs[0].start()
+    weights.start()
+    attend(1)
+    outs[1].start()
+    weights.partner()
     weights.step(1)
-    attend(1)
     outs[0].halves()
     outs[0].first(0)
     weights.step(2)
     attend(2)
+    outs[2].start()
     outs[0].first(1)
     outs[1].halves()
     outs[1].first(0)

time: 169 us -> 172 us (1.018)
  Pallas kernels: 158 us -> 162 us
    pallas_call x1, Pallas kernels: 47.5 us -> 58.5 us  [attend(): pl.pallas_call(attend_kernel, out_shape=jax.ShapeDtypeStruct(hidden.shape...]
    pallas_call x1, Pallas kernels: 111 us -> 104 us  [project(): pl.pallas_call(project_kernel, out_shape=(own, own, own, out(3 * tokens,...]
where the time goes in v4:
time: 172 us
  Pallas kernels  162 us (94%)
  local copies, waits for them, and re-layouts  7.35 us (4%)
  other arithmetic  2.16 us (1%)
    pallas_call x1, Pallas kernels, project(): pl.pallas_call(project_kernel, out_shape=(own, own, own, out(3 * tokens,...  104 us
    pallas_call x1, Pallas kernels, attend(): pl.pallas_call(attend_kernel, out_shape=jax.ShapeDtypeStruct(hidden.shape...  58.5 us
    unnamed x9, local copies, waits for them, and re-layouts  6.46 us

profile of v4, /device:TPU:1, one launch (start us, length us, event | category | flops | bytes accessed | tf_op | source)
XLA Modules:
  0.0 172.2 jit_solution(14549901173254964065)
XLA Ops:
  0.6 0.8 select_reduce_fusion
  1.4 0.7 add.15
  2.1 0.7 and_convert_fusion.onehot_ref
  2.8 0.9 slice.3
  3.7 0.8 copy.17
  4.5 2.1 %copy.15.hidden_ref = bf16[768,320]{1,0:T(8,128)(2,1)} copy(bf16[768,320]{0,1:T(8,128)(2,1)} %param.8) | data formatting | bytes 983040 | tf_op args[0]
  6.6 103.5 %project.1 = (bf16[768,256]{1,0:T(8,128)(2,1)}, bf16[768,256]{1,0:T(8,128)(2,1)}, bf16[768,256]{1,0:T(8,128)(2,1)}, bf16[2304,512]{1,0:T(8,128)(2,1)}, bf16[1024,512]{1,0:T(8,128)(2,1)}) custom-call(s32[4]{0:T(128)} %owner_ref.1, bf16[320,768]{1,0:T(8,128)(2,1)} %bitcast.5, bf16[2,320,48]{2,1,0:T(8,128)(2,1)} %bitcast.6, ...), custom_call_target="tpu_custom_call" | custom-call | tf_op jit(solution)/shard_map/project/pallas_call | solution.py:405
  110.1 0.0 copy-start.1
  110.1 0.0 copy-start
  110.2 58.5 %attend.1 = bf16[768,320]{1,0:T(8,128)(2,1)} custom-call(s32[48]{0:T(128)} %len_ref.1, s32[48]{0:T(128)} %group_ref.1, bf16[3,48,320]{2,1,0:T(8,128)(2,1)} %bitcast.7, bf16[320,256]{1,0:T(8,128)(2,1)} %bitcast.9, bf16[768,320]{1,0:T(8,128)(2,1)} %copy.15.hidden_ref, bf16[768,256]{1,0:T(8,128)(2,1)} %get-tuple-element.8.q_all, ...), custom_call_target="tpu_custom_call" | custom-call | tf_op jit(solution)/shard_map/attend/pallas_call | solution.py:527
  168.6 2.1 %copy.16 = bf16[768,320]{0,1:T(8,128)(2,1)} copy(bf16[768,320]{1,0:T(8,128)(2,1)} %attend.1) | data formatting | bytes 983040
  170.7 0.0 copy-done.1
  170.7 0.7 copy.20
  171.4 0.0 copy-done
  171.4 0.7 copy.21
  (1 shorter events, 0.0 us)
Async XLA Ops:
  110.1 60.6 %copy-start.1 = (bf16[768,256]{1,0:T(8,128)(2,1)S(1)}, bf16[768,256]{1,0:T(8,128)(2,1)}, u32[]{:S(2)}) copy-start(bf16[768,256]{1,0:T(8,128)(2,1)} %get-tuple-element.23) | copy-start | bytes 1179652
  110.1 61.3 %copy-start = (bf16[768,256]{1,0:T(8,128)(2,1)S(1)}, bf16[768,256]{1,0:T(8,128)(2,1)}, u32[]{:S(2)}) copy-start(bf16[768,256]{1,0:T(8,128)(2,1)} %get-tuple-element.24) | copy-start | bytes 1179652

commit v5 on v4

--- a/solution.py
+++ b/solution.py
@@ -254,22 +254,26 @@
 
 def project_kernel(
     owner_ref, hidden_ref, mod_ref, onehot_ref, w_ref, slot_ref, q_ref, k_ref, v_ref, near_ref, prefix_ref,
-    mod_all, w_all, acc, stats, pieces, send_sem, recv_sem,
+    mod_all, kv_all, wq_all, acc_kv, acc_q, stats, pieces, send_sem, recv_sem,
 ):
     at = Place()
     wire = Wire(send_sem, recv_sem)
     depth, tokens = hidden_ref.shape
-    width = w_ref.shape[1]
+    heads = w_ref.shape[1] // (3 * HD)
     groups = owner_ref.shape[0]
     piece = slot_ref.shape[0] // 16
-    rows = RowGather(at, wire, row_part(w_all, depth, 128), "w")
+    for_kv = RowGather(at, wire, row_part(kv_all, depth, 160), "kv")
+    for_q = RowGather(at, wire, row_part(wq_all, depth, 160), "q")
     shared = RowGather(at, wire, row_part(prefix_ref, groups * piece, groups * piece // 2), "p")
     cols = ColGather(at, wire, col_part(mod_all, depth), "m")
     row_devs = [((at.row + i) % 16, at.col) for i in range(16)]
     met = row_devs[1:] + [at.col_dev(i) for i in range(1, 16)]
     greet(met)
-    w_all[pl.ds(pl.multiple_of(at.row * depth, 16), depth), :] = w_ref[...]
-
+    own_rows = pl.ds(pl.multiple_of(at.row * depth, 16), depth)
+    for head in range(heads):
+        first = head * 3 * HD
+        wq_all[own_rows, head * HD : (head + 1) * HD] = w_ref[:, first : first + HD]
+        kv_all[own_rows, 2 * head * HD : 2 * (head + 1) * HD] = w_ref[:, first + HD : first + 3 * HD]
     hidden = hidden_ref[...].astype(jnp.float32)
     local_mean = jnp.sum(hidden, axis=0, keepdims=True) * (1.0 / depth)
     centred = hidden - local_mean
@@ -284,7 +288,7 @@
     meet(met)
     for i in range(1, 16):
         wire.send(("stat", i), stats.at[at.col], stats.at[at.col], at.col_dev(i))
-    rows.start()
+    for_kv.start()
 
     def piece_at(ref, index):
         return ref.at[pl.ds(pl.multiple_of(index * piece, 16), piece), :]
@@ -292,7 +296,7 @@
     for i in range(1, 16):
         wire.send(("slot", i), piece_at(slot_ref, (at.row + i) % 16), piece_at(pieces, at.row), row_devs[i])
     piece_at(pieces, at.row)[...] = piece_at(slot_ref, at.row)[...]
-    rows.partner()
+    for_kv.partner()
     for i in range(1, 16):
         wire.arrived(("stat", i), stats.at[(at.col - i + 16) % 16], at.col_dev(16 - i))
     means, squares = stats[:, 0:8, :], stats[:, 8:16, :]
@@ -305,8 +309,8 @@
         return jnp.concatenate([packed[j : j + 1, :] for j in range(spans)], axis=1)
 
     onehot = onehot_ref[...]
-    shift = jnp.dot(mod_ref[0], onehot, preferred_element_type=jnp.float32)
-    scale = jnp.dot(mod_ref[1], onehot, preferred_element_type=jnp.float32)
+    shift = contract_first(mod_ref[0], onehot)
+    scale = contract_first(mod_ref[1], onehot)
     modulated = (hidden_ref[...].astype(jnp.float32) - as_row(mean)) * as_row(inverse) * (1.0 + scale) + shift
     mod_all[pl.ds(pl.multiple_of(at.col * depth, 16), depth), :] = modulated.astype(jnp.bfloat16)
     cols.start()
@@ -319,47 +323,51 @@
         picks = jnp.where(from_slot == owner_ref[g] * piece + own_line, 1.0, 0.0).astype(jnp.bfloat16)
         chosen = jnp.dot(picks, pieces[...], preferred_element_type=jnp.float32).astype(jnp.bfloat16)
         prefix_ref[pl.ds(pl.multiple_of((at.row * groups + g) * piece, 16), piece), :] = chosen
-    shared.start()
-
-    def product(blocks, tile):
+
+    def product(weight, blocks, tile):
         starts = [pl.multiple_of(at.row_at(plane, dz) * depth, 16) for plane, dz in blocks]
         lanes = pl.ds(pl.multiple_of(tile * 256, 256), 256)
         left = jnp.concatenate([mod_all[pl.ds(s, depth), lanes] for s in starts], axis=0)
-        right = jnp.concatenate([w_all[pl.ds(s, depth), :] for s in starts], axis=0)
+        right = jnp.concatenate([weight[pl.ds(s, depth), :] for s in starts], axis=0)
         return contract_first(left, right)
 
-    def accumulate(blocks, fresh=False):
+    def accumulate(acc, weight, blocks, fresh=False):
         def one(tile, carry):
             at_rows = pl.ds(pl.multiple_of(tile * 256, 256), 256)
-            made = product(blocks, tile)
+            made = product(weight, blocks, tile)
             acc[at_rows, :] = made if fresh else acc[at_rows, :] + made
             return carry
 
         lax.fori_loop(0, tokens // 256, one, 0)
 
-    rows.step(1)
+    quarters = (
+        [(0, 0), (0, -1), (0, 1), (0, -2)],
+        [(0, 2), (0, -3), (0, 3), (1, 0)],
+        [(1, -1), (1, 1), (1, -2), (1, 2)],
+        [(0, 4), (1, -3), (1, 3), (1, 4)],
+    )
+    for_kv.step(1)
     cols.halves()
     cols.first(0)
-    shared.partner()
-    rows.step(2)
+    for_kv.step(2)
     cols.first(1)
     cols.second(0)
-    shared.step(1)
-    rows.step(3)
+    for_kv.step(3)
+    for_q.start()
     cols.second(1)
+    for_kv.step(4)
+    for_q.partner()
+    for_kv.from_x((0, -1, 1))
+    shared.start()
     cols.from_core()
-    shared.step(2)
-    accumulate([(0, 0), (0, -1), (0, 1), (0, -2)], True)
-    rows.step(4)
-    shared.step(3)
-    rows.from_x((0,))
-    accumulate([(0, 2), (0, -3), (0, 3), (1, 0)])
-    rows.from_x((-1, 1, -2, 2))
-    accumulate([(1, -1), (1, 1), (1, -2), (1, 2)])
-    shared.step(4)
-    rows.from_x((-3, 3, -4, 4))
-
-    heads = width // (3 * HD)
+    accumulate(acc_kv, kv_all, quarters[0], True)
+    for_q.step(1)
+    shared.partner()
+    accumulate(acc_kv, kv_all, quarters[1])
+    for_kv.from_x((-2, 2))
+    accumulate(acc_kv, kv_all, quarters[2])
+    for_kv.from_x((-3, 3, -4, 4))
+
     near = near_ref.shape[0]
     own = (near - tokens) // 2
     ahead, behind = ((at.row + 1) % 16, at.col), ((at.row + 15) % 16, at.col)
@@ -369,20 +377,34 @@
     spans_ahead, spans_behind = [], []
     for tile in range(tokens // 256):
         low, high = tile * 256, (tile + 1) * 256
-        made = (acc[low:high, :] + product([(0, 4), (1, -3), (1, 3), (1, 4)], tile)).astype(jnp.bfloat16)
+        made = (acc_kv[low:high, :] + product(kv_all, quarters[3], tile)).astype(jnp.bfloat16)
+        near_ref[own + low : own + high, :] = made
         for head in range(heads):
-            first = head * 3 * HD
             lanes = slice(head * HD, (head + 1) * HD)
-            q_ref[low:high, lanes] = made[:, first : first + HD]
-            k_ref[low:high, lanes] = made[:, first + HD : first + 2 * HD]
-            v_ref[low:high, lanes] = made[:, first + 2 * HD : first + 3 * HD]
-            near_ref[own + low : own + high, 2 * head * HD : 2 * (head + 1) * HD] = made[:, first + HD : first + 3 * HD]
+            k_ref[low:high, lanes] = made[:, 2 * head * HD : (2 * head + 1) * HD]
+            v_ref[low:high, lanes] = made[:, (2 * head + 1) * HD : (2 * head + 2) * HD]
         begin = max(low, tokens - HALO)
         spans_ahead.append((begin, high))
         wire.send(("up", tile), near_ref.at[own + begin : own + high, :], near_ref.at[begin - tokens + own : high - tokens + own, :], ahead)
         finish = min(high, HALO)
         spans_behind.append((low, finish))
         wire.send(("down", tile), near_ref.at[own + low : own + finish, :], near_ref.at[own + tokens + low : own + tokens + finish, :], behind)
+    for_q.step(2)
+    shared.step(1)
+    accumulate(acc_q, wq_all, quarters[0], True)
+    for_q.step(3)
+    shared.step(2)
+    for_q.from_x((0,))
+    accumulate(acc_q, wq_all, quarters[1])
+    for_q.step(4)
+    shared.step(3)
+    for_q.from_x((-1, 1, -2, 2))
+    accumulate(acc_q, wq_all, quarters[2])
+    shared.step(4)
+    for_q.from_x((-3, 3, -4, 4))
+    for tile in range(tokens // 256):
+        low, high = tile * 256, (tile + 1) * 256
+        q_ref[low:high, :] = (acc_q[low:high, :] + product(wq_all, quarters[3], tile)).astype(jnp.bfloat16)
     shared.from_x()
     for tile, (begin, high) in enumerate(spans_ahead):
         wire.arrived(("up", tile), near_ref.at[begin - tokens + own : high - tokens + own, :], behind)
@@ -391,7 +413,7 @@
     wire.drain()
 
 
-def project(owner, hidden_t, mod_t, onehot_t, w_qkv, slot):
+def project(owner, hidden_t, mod, onehot_t, w_qkv, slot):
     depth, tokens = hidden_t.shape
     width = w_qkv.shape[1]
     groups, slot_len = owner.shape[0], slot.shape[0]
@@ -409,16 +431,18 @@
         out_specs=(vmem,) * 5,
         scratch_shapes=[
             pltpu.VMEM((16 * depth, tokens), jnp.bfloat16),
-            pltpu.VMEM((16 * depth, width), jnp.bfloat16),
-            pltpu.VMEM((tokens, width), jnp.float32),
+            pltpu.VMEM((16 * depth, 2 * heads * HD), jnp.bfloat16),
+            pltpu.VMEM((16 * depth, heads * HD), jnp.bfloat16),
+            pltpu.VMEM((tokens, 2 * heads * HD), jnp.float32),
+            pltpu.VMEM((tokens, heads * HD), jnp.float32),
             pltpu.VMEM((16, 16, 128), jnp.float32),
             pltpu.VMEM((slot_len, 2 * heads * HD), jnp.bfloat16),
-            pltpu.SemaphoreType.DMA((128,)),
-            pltpu.SemaphoreType.DMA((128,)),
+            pltpu.SemaphoreType.DMA((160,)),
+            pltpu.SemaphoreType.DMA((160,)),
         ],
         compiler_params=pltpu.CompilerParams(collective_id=0, has_side_effects=True, vmem_limit_bytes=VMEM_LIMIT),
         name="project",
-    )(owner, hidden_t, mod_t, onehot_t, w_qkv, slot)
+    )(owner, hidden_t, mod, onehot_t, w_qkv, slot)
 
 
 def attend_kernel(
@@ -502,15 +526,15 @@
     outs[2].first(1)
     outs[1].second(1)
     weights.from_x()
-    gate = contract_first(onehot, mod_ref[2])
+    gate = contract_first(mod_ref[2], onehot)
     right = jnp.concatenate([w_out_all[j * features : (j + 1) * features, :] for j in range(16)], axis=1)
 
     def finish_tile(t):
         low, high = t * TILE, (t + 1) * TILE
         outs[t].from_core()
         left = jnp.concatenate([att_all[j * tokens + low : j * tokens + high, :] for j in range(16)], axis=1)
-        made = lax.dot_general(left, right, (((1,), (1,)), ((), ())), preferred_element_type=jnp.float32)
-        out_ref[low:high, :] = (hidden_ref[low:high, :].astype(jnp.float32) + gate[low:high, :] * made).astype(jnp.bfloat16)
+        made = lax.dot_general(right, left, (((1,), (1,)), ((), ())), preferred_element_type=jnp.float32)
+        out_ref[:, low:high] = (hidden_ref[:, low:high].astype(jnp.float32) + gate[:, low:high] * made).astype(jnp.bfloat16)
 
     finish_tile(0)
     outs[2].second(0)
@@ -522,7 +546,7 @@
 
 def attend(req_len, req_group, mod, w_out_t, hidden, q, near, prefix):
     tokens, own = q.shape
-    features = hidden.shape[1]
+    features = hidden.shape[0]
     vmem = pl.BlockSpec(memory_space=pltpu.VMEM)
     return pl.pallas_call(
         attend_kernel,
@@ -552,13 +576,13 @@
     place = first + jnp.arange(tokens, dtype=jnp.int32)
     inside = (starts[:, None] <= place[None, :]) & (place[None, :] < ends[:, None])
     onehot_t = inside.astype(jnp.bfloat16)
-    mod_t = jnp.transpose(modulation[:, :2], (1, 2, 0))
+    mod = jnp.transpose(modulation, (1, 0, 2))
+    hidden_t = jnp.transpose(hidden_in)
     q, new_keys, new_values, near, prefix = project(
-        owner, jnp.transpose(hidden_in), mod_t, onehot_t, w_qkv, prefix_cache[0]
+        owner, hidden_t, mod, onehot_t, w_qkv, prefix_cache[0]
     )
-    mod = jnp.transpose(modulation, (1, 0, 2))
-    hidden_out = attend(req_len, req_group, mod, jnp.transpose(w_out), hidden_in, q, near, prefix)
-    return hidden_out, new_keys, new_values
+    hidden_out = attend(req_len, req_group, mod, jnp.transpose(w_out), hidden_t, q, near, prefix)
+    return jnp.transpose(hidden_out), new_keys, new_values
 
 
 def solution(mesh):

time: 172 us -> 166 us (0.965)
  local copies, waits for them, and re-layouts: 7.35 us -> 3.34 us
  Pallas kernels: 162 us -> 160 us
    pallas_call x1, Pallas kernels: 58.5 us -> 53.6 us  [attend(): pl.pallas_call(attend_kernel, out_shape=jax.ShapeDtypeStruct(hidden.shape...]
    unnamed x9 -> x7, local copies, waits for them, and re-layouts: 6.46 us -> 3.34 us
    pallas_call x1, Pallas kernels: 104 us -> 106 us  [project(): pl.pallas_call(project_kernel, out_shape=(own, own, own, out(3 * tokens,...]
where the time goes in v5:
time: 166 us
  Pallas kernels  160 us (96%)
  local copies, waits for them, and re-layouts  3.34 us (2%)
  other arithmetic  2.16 us (1%)
    pallas_call x1, Pallas kernels, project(): pl.pallas_call(project_kernel, out_shape=(own, own, own, out(3 * tokens,...  106 us
    pallas_call x1, Pallas kernels, attend(): pl.pallas_call(attend_kernel, out_shape=jax.ShapeDtypeStruct(hidden.shape...  53.6 us
    unnamed x7, local copies, waits for them, and re-layouts  3.34 us

profile of v5, /device:TPU:1, one launch (start us, length us, event | category | flops | bytes accessed | tf_op | source)
XLA Modules:
  0.0 165.7 jit_solution(554094569811896986)
XLA Ops:
  0.6 0.8 select_reduce_fusion
  1.4 0.7 add.15
  2.1 0.7 and_convert_fusion.onehot_ref
  2.8 106.0 %project.1 = (bf16[768,256]{1,0:T(8,128)(2,1)}, bf16[768,256]{1,0:T(8,128)(2,1)}, bf16[768,256]{1,0:T(8,128)(2,1)}, bf16[2304,512]{1,0:T(8,128)(2,1)}, bf16[1024,512]{1,0:T(8,128)(2,1)}) custom-call(s32[4]{0:T(128)} %owner_ref.1, bf16[320,768]{1,0:T(8,128)(2,1)} %bitcast.6, bf16[3,48,320]{2,1,0:T(8,128)(2,1)} %bitcast.8, ...), custom_call_target="tpu_custom_call" | custom-call | tf_op jit(solution)/shard_map/project/pallas_call | solution.py:427
  108.8 0.0 copy-start.1
  108.8 0.0 copy-start
  108.8 53.6 %attend.1 = bf16[320,768]{1,0:T(8,128)(2,1)} custom-call(s32[48]{0:T(128)} %len_ref.1, s32[48]{0:T(128)} %group_ref.1, bf16[3,48,320]{2,1,0:T(8,128)(2,1)} %bitcast.9, bf16[320,256]{1,0:T(8,128)(2,1)} %bitcast.11, bf16[320,768]{1,0:T(8,128)(2,1)} %bitcast.7, bf16[768,256]{1,0:T(8,128)(2,1)} %get-tuple-element.8.q_all, ...), custom_call_target="tpu_custom_call" | custom-call | tf_op jit(solution)/shard_map/attend/pallas_call | solution.py:551
  162.4 1.8 %copy.14 = bf16[768,320]{0,1:T(8,128)(2,1)} copy(bf16[768,320]{0,1:T(8,128)(2,1)} %bitcast.5) | data formatting | bytes 983040
  164.2 0.0 copy-done.1
  164.2 0.7 copy.15
  165.0 0.0 copy-done
  165.0 0.7 copy.16
  (1 shorter events, 0.0 us)
Async XLA Ops:
  108.8 55.5 %copy-start.1 = (bf16[768,256]{1,0:T(8,128)(2,1)S(1)}, bf16[768,256]{1,0:T(8,128)(2,1)}, u32[]{:S(2)}) copy-start(bf16[768,256]{1,0:T(8,128)(2,1)} %get-tuple-element.17) | copy-start | bytes 1179652
  108.8 56.2 %copy-start = (bf16[768,256]{1,0:T(8,128)(2,1)S(1)}, bf16[768,256]{1,0:T(8,128)(2,1)}, u32[]{:S(2)}) copy-start(bf16[768,256]{1,0:T(8,128)(2,1)} %get-tuple-element.18) | copy-start | bytes 1179652

commit v6 on v5

--- a/solution.py
+++ b/solution.py
@@ -505,24 +505,24 @@
     weights.start()
     attend(1)
     outs[1].start()
+    outs[0].halves()
     weights.partner()
-    weights.step(1)
-    outs[0].halves()
     outs[0].first(0)
-    weights.step(2)
     attend(2)
     outs[2].start()
     outs[0].first(1)
+    weights.step(1)
     outs[1].halves()
     outs[1].first(0)
-    weights.step(3)
+    weights.step(2)
     outs[0].second(0)
     outs[1].first(1)
     outs[2].halves()
+    weights.step(3)
     outs[0].second(1)
     outs[2].first(0)
+    outs[1].second(0)
     weights.step(4)
-    outs[1].second(0)
     outs[2].first(1)
     outs[1].second(1)
     weights.from_x()

time: 166 us -> 161 us (0.970)
  Pallas kernels: 160 us -> 154 us
    pallas_call x1, Pallas kernels: 53.6 us -> 48.4 us  [attend(): pl.pallas_call(attend_kernel, out_shape=jax.ShapeDtypeStruct(hidden.shape...]
where the time goes in v6:
time: 161 us
  Pallas kernels  154 us (96%)
  local copies, waits for them, and re-layouts  3.34 us (2%)
  other arithmetic  2.16 us (1%)
    pallas_call x1, Pallas kernels, project(): pl.pallas_call(project_kernel, out_shape=(own, own, own, out(3 * tokens,...  106 us
    pallas_call x1, Pallas kernels, attend(): pl.pallas_call(attend_kernel, out_shape=jax.ShapeDtypeStruct(hidden.shape...  48.4 us
    unnamed x7, local copies, waits for them, and re-layouts  3.34 us

profile of v6, /device:TPU:1, one launch (start us, length us, event | category | flops | bytes accessed | tf_op | source)
XLA Modules:
  0.0 160.6 jit_solution(15631053030748176330)
XLA Ops:
  0.6 0.8 select_reduce_fusion
  1.4 0.7 add.15
  2.1 0.7 and_convert_fusion.onehot_ref
  2.8 106.0 %project.1 = (bf16[768,256]{1,0:T(8,128)(2,1)}, bf16[768,256]{1,0:T(8,128)(2,1)}, bf16[768,256]{1,0:T(8,128)(2,1)}, bf16[2304,512]{1,0:T(8,128)(2,1)}, bf16[1024,512]{1,0:T(8,128)(2,1)}) custom-call(s32[4]{0:T(128)} %owner_ref.1, bf16[320,768]{1,0:T(8,128)(2,1)} %bitcast.6, bf16[3,48,320]{2,1,0:T(8,128)(2,1)} %bitcast.8, ...), custom_call_target="tpu_custom_call" | custom-call | tf_op jit(solution)/shard_map/project/pallas_call | solution.py:427
  108.8 0.0 copy-start.1
  108.8 0.0 copy-start
  108.8 48.4 %attend.1 = bf16[320,768]{1,0:T(8,128)(2,1)} custom-call(s32[48]{0:T(128)} %len_ref.1, s32[48]{0:T(128)} %group_ref.1, bf16[3,48,320]{2,1,0:T(8,128)(2,1)} %bitcast.9, bf16[320,256]{1,0:T(8,128)(2,1)} %bitcast.11, bf16[320,768]{1,0:T(8,128)(2,1)} %bitcast.7, bf16[768,256]{1,0:T(8,128)(2,1)} %get-tuple-element.8.q_all, ...), custom_call_target="tpu_custom_call" | custom-call | tf_op jit(solution)/shard_map/attend/pallas_call | solution.py:551
  157.2 1.8 %copy.14 = bf16[768,320]{0,1:T(8,128)(2,1)} copy(bf16[768,320]{0,1:T(8,128)(2,1)} %bitcast.5) | data formatting | bytes 983040
  159.1 0.0 copy-done.1
  159.1 0.7 copy.15
  159.8 0.0 copy-done
  159.8 0.7 copy.16
  (1 shorter events, 0.0 us)
Async XLA Ops:
  108.8 50.3 %copy-start.1 = (bf16[768,256]{1,0:T(8,128)(2,1)S(1)}, bf16[768,256]{1,0:T(8,128)(2,1)}, u32[]{:S(2)}) copy-start(bf16[768,256]{1,0:T(8,128)(2,1)} %get-tuple-element.17) | copy-start | bytes 1179652
  108.8 51.0 %copy-start = (bf16[768,256]{1,0:T(8,128)(2,1)S(1)}, bf16[768,256]{1,0:T(8,128)(2,1)}, u32[]{:S(2)}) copy-start(bf16[768,256]{1,0:T(8,128)(2,1)} %get-tuple-element.18) | copy-start | bytes 1179652
